TPU v7x, 32 devices: a whole 2x2x4 slice. The times are simulated.
32 devices in a mesh: ctx: 8 (over z, y), dp: 4 (over x, core).
Axes of the slice: x: 2, y: 2, z: 4, core: 2. Of those that a mesh axis runs over, the one named last changes fastest.
Arguments:
- tokens: bfloat16 [8, 1024, 1536], P('dp', 'ctx'), may hold values from -6 to 6
- block_pair: int32 [8], replicated, may hold values from 0 to 7, each once
- gain_attn: bfloat16 [1536], P('dp'), may hold values from 0.099609375 to 1.8984375
- w_query: bfloat16 [1536, 1536], P('dp'), may hold values from -0.15625 to 0.15625
- b_query: bfloat16 [1536], P('dp'), may hold values from -2.5 to 2.5
- w_key: bfloat16 [1536, 256], P('dp'), may hold values from -0.15625 to 0.15625
- b_key: bfloat16 [256], P('dp'), may hold values from -2.5 to 2.5
- w_value: bfloat16 [1536, 256], P('dp'), may hold values from -0.15625 to 0.15625
- b_value: bfloat16 [256], P('dp'), may hold values from -0.59765625 to 0.59765625
- w_out: bfloat16 [1536, 1536], P('dp'), may hold values from -0.875 to 0.875
- gain_mlp: bfloat16 [1536], P('dp'), may hold values from 0.099609375 to 1.8984375
- w_gate: bfloat16 [1536, 8960], P(None, 'dp'), may hold values from -0.15625 to 0.15625
- w_up: bfloat16 [1536, 8960], P(None, 'dp'), may hold values from -0.15625 to 0.15625
- w_down: bfloat16 [8960, 1536], P('dp'), may hold values from -0.0625 to 0.0625
- cotangent: bfloat16 [8, 1024, 1536], P('dp', 'ctx'), may hold values from -6 to 6
Outputs:
- layer_out: bfloat16 [8, 1024, 1536], P('dp', 'ctx')
- grad_input: float32 [8, 1024, 1536], P('dp', 'ctx')
- grad_gain_attn: float32 [1536], P('dp')
- grad_w_query: float32 [1536, 1536], P('dp')
- grad_b_query: float32 [1536], P('dp')
- grad_w_key: float32 [1536, 256], P('dp')
- grad_b_key: float32 [256], P('dp')
- grad_w_value: float32 [1536, 256], P('dp')
- grad_b_value: float32 [256], P('dp')
- grad_w_out: float32 [1536, 1536], P('dp')
- grad_gain_mlp: float32 [1536], P('dp')
- grad_w_gate: float32 [1536, 8960], P(None, 'dp')
- grad_w_up: float32 [1536, 8960], P(None, 'dp')
- grad_w_down: float32 [8960, 1536], P('dp')
Inputs may be any that keep to these rules, and one draw needn't show every extreme that they name: A permutation; index c of ctx holds blocks block_pair[c] and 15 - block_pair[c] of every sequence.
All inputs are finite; a program needn't handle non-finite values.
Results may differ from a plain program's by a relative error of at most 0.02.
Values may be sent and summed in bfloat16 or wider, within the bound.
No kernel may reach another device: no remote copies, remote signals or barrier semaphores. Data moves between devices by JAX's collectives and lax.ppermute only.
A program may use at most 512 MiB of HBM per device.

v0:
```python
import math

import jax
import jax.numpy as jnp
from jax import lax
from jax.sharding import PartitionSpec as P

HEADS = 12
KV_HEADS = 2
HEAD = 128


EPSILON = 1e-06
THETA = 1000000.0


def matmul(left, right, left_dim, right_dim):
    return lax.dot_general(
        left, right, (((left_dim,), (right_dim,)), ((), ())), preferred_element_type=jnp.float32
    )


def block_positions(block_pair, n_ctx, seq_tok):
    half_blk = seq_tok // 2
    row_ids = jnp.arange(n_ctx * seq_tok, dtype=jnp.int32)
    owner = row_ids // seq_tok
    within = row_ids % seq_tok
    matches = owner[:, None] == jnp.arange(n_ctx, dtype=jnp.int32)[None, :]
    first = jnp.sum(jnp.where(matches, block_pair[None, :], 0), 1)
    chosen = jnp.where(within < half_blk, first, 2 * n_ctx - 1 - first)
    return chosen * half_blk + within % half_blk


def angles_for(positions, head_size):
    half_size = head_size // 2
    freqs = jnp.exp(jnp.arange(half_size, dtype=jnp.float32) * (-math.log(THETA) / half_size))
    angle = positions.astype(jnp.float32)[:, None] * freqs[None, :]
    return (jnp.cos(angle), jnp.sin(angle))


def rotate(vectors, cosine, sine):
    half_size = vectors.shape[-1] // 2
    front = vectors[..., :half_size]
    behind = vectors[..., half_size:]
    return jnp.concatenate([front * cosine - behind * sine, behind * cosine + front * sine], -1)


def rms_scale(vectors):
    return lax.rsqrt(jnp.mean(vectors * vectors, -1, keepdims=True) + EPSILON)


def rms_back(grad_norm, vectors, scale, gain):
    weighted = grad_norm * gain
    grad_vectors = scale * weighted - vectors * scale**3 * jnp.mean(
        weighted * vectors, -1, keepdims=True
    )
    grad_gain = jnp.sum(grad_norm * vectors * scale, 0)
    return (grad_vectors, grad_gain)


def scores_of(queries, key_rows, query_pos, key_pos):
    scale = queries.shape[-1] ** (-0.5)
    scores = (
        jnp.einsum("nkgd,lkd->kgnl", queries, key_rows, preferred_element_type=jnp.float32) * scale
    )
    allowed = key_pos[None, :] <= query_pos[:, None]
    return jnp.where(allowed[None, None], scores, -jnp.inf)


def attend_forward(queries, key_rows, value_rows, query_pos, key_pos):
    scores = scores_of(queries, key_rows, query_pos, key_pos)
    highest = jnp.max(scores, -1, keepdims=True)
    expon = jnp.exp(scores - highest)
    denom = jnp.sum(expon, -1, keepdims=True)
    probs = (expon / denom).astype(jnp.bfloat16)
    mixed = jnp.einsum("kgnl,lkd->nkgd", probs, value_rows, preferred_element_type=jnp.float32)
    return (mixed, highest + jnp.log(denom))


def attend_backward(queries, key_rows, value_rows, query_pos, key_pos, log_sum, grad_mixed):
    scale = queries.shape[-1] ** (-0.5)
    probs = jnp.exp(scores_of(queries, key_rows, query_pos, key_pos) - log_sum)
    grad_values = jnp.einsum(
        "kgnl,nkgd->lkd", probs.astype(jnp.bfloat16), grad_mixed, preferred_element_type=jnp.float32
    )
    grad_probs = jnp.einsum(
        "nkgd,lkd->kgnl", grad_mixed, value_rows, preferred_element_type=jnp.float32
    )
    centre = jnp.sum(probs * grad_probs, -1, keepdims=True)
    grad_scores = (probs * (grad_probs - centre)).astype(jnp.bfloat16)
    grad_queries = (
        jnp.einsum("kgnl,lkd->nkgd", grad_scores, key_rows, preferred_element_type=jnp.float32)
        * scale
    )
    grad_keys = (
        jnp.einsum("kgnl,nkgd->lkd", grad_scores, queries, preferred_element_type=jnp.float32)
        * scale
    )
    return (grad_queries, grad_keys, grad_values)


def mlp_forward(normed, gate_weight, up_weight):
    gate = matmul(normed, gate_weight, 1, 0)
    up_proj = matmul(normed, up_weight, 1, 0)
    return (gate, up_proj, (jax.nn.silu(gate) * up_proj).astype(jnp.bfloat16))


def mlp_back(grad_rows, gate, up_proj, down_weight):
    grad_hidden = matmul(grad_rows, down_weight, 1, 1)
    sigma = jax.nn.sigmoid(gate)
    grad_gate = (grad_hidden * up_proj * sigma * (1.0 + gate * (1.0 - sigma))).astype(jnp.bfloat16)
    grad_up = (grad_hidden * gate * sigma).astype(jnp.bfloat16)
    return (grad_gate, grad_up)


def shards(
    tokens,
    block_pair,
    gain_attn,
    w_query,
    b_query,
    w_key,
    b_key,
    w_value,
    b_value,
    w_out,
    gain_mlp,
    w_gate,
    w_up,
    w_down,
    cotangent,
):
    n_ctx = lax.axis_size("ctx")
    seq_grp, seq_tok, width = tokens.shape
    group = HEADS // KV_HEADS
    kv_width = KV_HEADS * HEAD
    total_rows = seq_grp * seq_tok
    key_pos = block_positions(block_pair, n_ctx, seq_tok)
    query_pos = lax.dynamic_slice_in_dim(key_pos, lax.axis_index("ctx") * seq_tok, seq_tok)
    cosine, sine = angles_for(query_pos, HEAD)
    cosine = cosine[None, :, None, :]
    sine = sine[None, :, None, :]
    gain_a, full_query, bias_query, full_key, bias_key, full_value, bias_value, full_out, gain_m = (
        lax.all_gather(gain_attn, "dp", axis=0, tiled=True),
        lax.all_gather(w_query, "dp", axis=0, tiled=True),
        lax.all_gather(b_query, "dp", axis=0, tiled=True),
        lax.all_gather(w_key, "dp", axis=0, tiled=True),
        lax.all_gather(b_key, "dp", axis=0, tiled=True),
        lax.all_gather(w_value, "dp", axis=0, tiled=True),
        lax.all_gather(b_value, "dp", axis=0, tiled=True),
        lax.all_gather(w_out, "dp", axis=0, tiled=True),
        lax.all_gather(gain_mlp, "dp", axis=0, tiled=True),
    )
    gain_one = gain_a.astype(jnp.float32)
    gain_two = gain_m.astype(jnp.float32)
    inputs = tokens.astype(jnp.float32).reshape(total_rows, width)
    scale_one = rms_scale(inputs)
    normed_one = (inputs * scale_one * gain_one).astype(jnp.bfloat16)
    query_pre = matmul(normed_one, full_query, 1, 0) + bias_query.astype(jnp.float32)
    key_pre = matmul(normed_one, full_key, 1, 0) + bias_key.astype(jnp.float32)
    value_pre = matmul(normed_one, full_value, 1, 0) + bias_value.astype(jnp.float32)
    queries = rotate(query_pre.reshape(seq_grp, seq_tok, HEADS, HEAD), cosine, sine).astype(
        jnp.bfloat16
    )
    keys_own = rotate(key_pre.reshape(seq_grp, seq_tok, KV_HEADS, HEAD), cosine, sine).astype(
        jnp.bfloat16
    )
    values_own = value_pre.reshape(seq_grp, seq_tok, KV_HEADS, HEAD).astype(jnp.bfloat16)
    keys_all, values_all = (
        lax.all_gather(keys_own, "ctx", axis=1, tiled=True),
        lax.all_gather(values_own, "ctx", axis=1, tiled=True),
    )
    grouped = queries.reshape(seq_grp, seq_tok, KV_HEADS, group, HEAD)

    def forward_one(items):
        return attend_forward(items[0], items[1], items[2], query_pos, key_pos)

    mixed, log_sum = lax.map(forward_one, (grouped, keys_all, values_all))
    attn_vec = mixed.reshape(total_rows, width).astype(jnp.bfloat16)
    middle = inputs + matmul(attn_vec, full_out, 1, 0)
    scale_two = rms_scale(middle)
    normed_two = (middle * scale_two * gain_two).astype(jnp.bfloat16)
    grad_top = cotangent.reshape(total_rows, width)
    full_gate, full_up, full_down = (
        lax.all_gather(w_gate, "dp", axis=1, tiled=True),
        lax.all_gather(w_up, "dp", axis=1, tiled=True),
        lax.all_gather(w_down, "dp", axis=0, tiled=True),
    )
    gate, up_proj, hidden = mlp_forward(normed_two, full_gate, full_up)
    mlp_out = matmul(hidden, full_down, 1, 0)
    grad_gate, grad_up = mlp_back(grad_top, gate, up_proj, full_down)
    grad_norm_two = matmul(grad_gate, full_gate, 1, 1) + matmul(grad_up, full_up, 1, 1)
    grad_w_gate, grad_w_up, grad_w_down = (
        lax.psum_scatter(
            matmul(normed_two, grad_gate, 0, 0), "dp", scatter_dimension=1, tiled=True
        ),
        lax.psum_scatter(matmul(normed_two, grad_up, 0, 0), "dp", scatter_dimension=1, tiled=True),
        lax.psum_scatter(matmul(hidden, grad_top, 0, 0), "dp", scatter_dimension=0, tiled=True),
    )
    layer_out = (middle + mlp_out).astype(jnp.bfloat16).reshape(tokens.shape)
    grad_middle_norm, grad_gain_m = rms_back(grad_norm_two, middle, scale_two, gain_two)
    grad_middle = grad_top.astype(jnp.float32) + grad_middle_norm
    grad_branch = grad_middle.astype(jnp.bfloat16)
    grad_w_out = matmul(attn_vec, grad_branch, 0, 0)
    grad_attn = matmul(grad_branch, full_out, 1, 1).astype(jnp.bfloat16)
    grad_mixed = grad_attn.reshape(seq_grp, seq_tok, KV_HEADS, group, HEAD)

    def backward_one(items):
        return attend_backward(items[0], items[1], items[2], query_pos, key_pos, items[3], items[4])

    grad_queries, grad_keys_all, grad_values_all = lax.map(
        backward_one, (grouped, keys_all, values_all, log_sum, grad_mixed)
    )
    grad_keys, grad_values = (
        lax.psum_scatter(grad_keys_all, "ctx", scatter_dimension=1, tiled=True),
        lax.psum_scatter(grad_values_all, "ctx", scatter_dimension=1, tiled=True),
    )
    grad_query_pre = (
        rotate(grad_queries.reshape(seq_grp, seq_tok, HEADS, HEAD), cosine, -sine)
        .reshape(total_rows, width)
        .astype(jnp.bfloat16)
    )
    grad_key_pre = (
        rotate(grad_keys, cosine, -sine).reshape(total_rows, kv_width).astype(jnp.bfloat16)
    )
    grad_value_pre = grad_values.reshape(total_rows, kv_width).astype(jnp.bfloat16)
    grad_w_query = matmul(normed_one, grad_query_pre, 0, 0)
    grad_w_key = matmul(normed_one, grad_key_pre, 0, 0)
    grad_w_value = matmul(normed_one, grad_value_pre, 0, 0)
    grad_b_query = jnp.sum(grad_query_pre.astype(jnp.float32), 0)
    grad_b_key = jnp.sum(grad_key_pre.astype(jnp.float32), 0)
    grad_b_value = jnp.sum(grad_value_pre.astype(jnp.float32), 0)
    grad_norm_one = (
        matmul(grad_query_pre, full_query, 1, 1)
        + matmul(grad_key_pre, full_key, 1, 1)
        + matmul(grad_value_pre, full_value, 1, 1)
    )
    grad_in_norm, grad_gain_a = rms_back(grad_norm_one, inputs, scale_one, gain_one)
    grad_input = (grad_middle + grad_in_norm).reshape(tokens.shape)
    (
        shard_gain_a,
        shard_query,
        shard_b_query,
        shard_key,
        shard_b_key,
        shard_value,
        shard_b_value,
        shard_out,
        shard_gain_m,
    ) = (
        lax.psum_scatter(grad_gain_a, "dp", scatter_dimension=0, tiled=True),
        lax.psum_scatter(grad_w_query, "dp", scatter_dimension=0, tiled=True),
        lax.psum_scatter(grad_b_query, "dp", scatter_dimension=0, tiled=True),
        lax.psum_scatter(grad_w_key, "dp", scatter_dimension=0, tiled=True),
        lax.psum_scatter(grad_b_key, "dp", scatter_dimension=0, tiled=True),
        lax.psum_scatter(grad_w_value, "dp", scatter_dimension=0, tiled=True),
        lax.psum_scatter(grad_b_value, "dp", scatter_dimension=0, tiled=True),
        lax.psum_scatter(grad_w_out, "dp", scatter_dimension=0, tiled=True),
        lax.psum_scatter(grad_gain_m, "dp", scatter_dimension=0, tiled=True),
    )
    summed = lax.psum(
        (
            shard_gain_a,
            shard_query,
            shard_b_query,
            shard_key,
            shard_b_key,
            shard_value,
            shard_b_value,
            shard_out,
            shard_gain_m,
            grad_w_gate,
            grad_w_up,
            grad_w_down,
        ),
        "ctx",
    )
    return (
        layer_out,
        grad_input,
        summed[0],
        summed[1],
        summed[2],
        summed[3],
        summed[4],
        summed[5],
        summed[6],
        summed[7],
        summed[8],
        summed[9],
        summed[10],
        summed[11],
    )


def solution(mesh):
    placed = (
        P("dp", "ctx", None),
        P(),
        P("dp"),
        P("dp", None),
        P("dp"),
        P("dp", None),
        P("dp"),
        P("dp", None),
        P("dp"),
        P("dp", None),
        P("dp"),
        P(None, "dp"),
        P(None, "dp"),
        P("dp", None),
        P("dp", "ctx", None),
    )
    return jax.shard_map(
        shards,
        mesh=mesh,
        in_specs=placed,
        out_specs=(
            P("dp", "ctx", None),
            P("dp", "ctx", None),
            P("dp"),
            P("dp", None),
            P("dp"),
            P("dp", None),
            P("dp"),
            P("dp", None),
            P("dp"),
            P("dp", None),
            P("dp"),
            P(None, "dp"),
            P(None, "dp"),
            P("dp", None),
        ),
        check_vma=False,
    )
```

profile of v0, /device:TPU:8, one launch (start us, length us, event | category | flops | bytes accessed | tf_op | source)
XLA Modules:
  0.0 3778.7 jit_solution(7601237029936238472)
XLA Ops:
  81.1 37.0 all-gather.15.cloned.1.call-done
  129.5 30.6 all-gather.11.cloned.1.call-done
  173.1 25.6 all-gather.17.cloned.1.call-done
  203.9 164.1 %all-gather.19.cloned.1.call-done = bf16[1536,8960]{0,1:T(8,128)(2,1)} async-done(((bf16[1536,2240]{0,1:T(8,128)(2,1)}), bf16[1536,8960]{0,1:T(8,128)(2,1)}) %all-gather.19.cloned.1.call-update) | async-done | bytes 27525136 | tf_op jit(solution)/shard_map/all_gather | solution.py:185
  368.0 19.9 fusion.107
  387.9 149.4 %all-gather.21.cloned.1.call-done = bf16[1536,8960]{0,1:T(8,128)(2,1)} async-done(((bf16[1536,2240]{0,1:T(8,128)(2,1)}), bf16[1536,8960]{0,1:T(8,128)(2,1)}) %all-gather.21.cloned.1.call-update) | async-done | bytes 27525136 | tf_op jit(solution)/shard_map/all_gather | solution.py:186
  537.3 19.0 fusion.108
  556.3 150.5 %all-gather.23.cloned.1.call-done = bf16[8960,1536]{1,0:T(8,128)(2,1)} async-done(((bf16[2240,1536]{1,0:T(8,128)(2,1)}), bf16[8960,1536]{1,0:T(8,128)(2,1)}) %all-gather.23.cloned.1.call-update) | async-done | bytes 27525136 | tf_op jit(solution)/shard_map/all_gather | solution.py:187
  706.8 20.1 multiply_convert_fusion
  764.7 75.8 %while.27 = (s32[]{:T(128)}, f32[2,128,2,6,128]{1,0,4,3,2:T(2,128)}, f32[2,1024,2,128]{1,3,2,0:T(8,128)}, f32[2,1024,2,128]{1,3,2,0:T(8,128)}, bf16[2,1024,2,128...) while((s32[]{:T(128)}, ...), condition=%wide.region_10.11_spmd, body=%wide.region_8.10_spmd.sunk | while | flops 2037447168 | bytes 122477496 | solution.py:211
  773.1 20.4 dynamic_update_slice.31
  810.9 20.4 dynamic_update_slice.31
  841.9 66.2 %reduce-scatter.10.cloned.1.call-done = f32[2,128,2,128]{1,3,2,0:T(8,128)} async-done(((f32[2,1024,2,128]{1,3,2,0:T(8,128)}), f32[2,128,2,128]{1,3,2,0:T(8,128)}) %reduce-scatter.10.cloned.1.call-update) | async-done | bytes 262160 | tf_op jit(solution)/shard_map/reduce_scatter | solution.py:215
  911.0 68.3 %reduce-scatter.12.cloned.1.call-done = f32[2,128,2,128]{1,3,2,0:T(8,128)} async-done(((f32[2,1024,2,128]{1,3,2,0:T(8,128)}), f32[2,128,2,128]{1,3,2,0:T(8,128)}) %reduce-scatter.12.cloned.1.call-update) | async-done | bytes 262160 | tf_op jit(solution)/shard_map/reduce_scatter | solution.py:216
  1002.3 23.1 fusion.110
  1025.7 22.4 fusion.111
  1049.2 26.1 fusion.112
  1075.4 47.6 %reduce-scatter.14.cloned.1.call-done = f32[384,1536]{1,0:T(8,128)} async-done(((f32[1536,1536]{1,0:T(8,128)}), f32[384,1536]{1,0:T(8,128)}) %reduce-scatter.14.cloned.1.call-update) | async-done | bytes 2359312 | tf_op jit(solution)/shard_map/reduce_scatter | solution.py:252
  1123.1 81.7 %reduce-scatter.20.cloned.1.call-done = f32[384,1536]{1,0:T(8,128)} async-done(((f32[1536,1536]{1,0:T(8,128)}), f32[384,1536]{1,0:T(8,128)}) %reduce-scatter.20.cloned.1.call-update) | async-done | bytes 2359312 | tf_op jit(solution)/shard_map/reduce_scatter | solution.py:258
  1204.7 376.3 %reduce-scatter.22.cloned.1.call-done = f32[1536,2240]{0,1:T(8,128)} async-done(((f32[1536,8960]{0,1:T(8,128)}), f32[1536,2240]{0,1:T(8,128)}) %reduce-scatter.22.cloned.1.call-update) | async-done | bytes 13762576 | tf_op jit(solution)/shard_map/reduce_scatter | solution.py:194
  1581.1 376.5 %reduce-scatter.24.cloned.1.call-done = f32[1536,2240]{0,1:T(8,128)} async-done(((f32[1536,8960]{0,1:T(8,128)}), f32[1536,2240]{0,1:T(8,128)}) %reduce-scatter.24.cloned.1.call-update) | async-done | bytes 13762576 | tf_op jit(solution)/shard_map/reduce_scatter | solution.py:197
  1957.6 376.3 %reduce-scatter.26.cloned.1.call-done = f32[2240,1536]{1,0:T(8,128)} async-done(((f32[8960,1536]{1,0:T(8,128)}), f32[2240,1536]{1,0:T(8,128)}) %reduce-scatter.26.cloned.1.call-update) | async-done | bytes 13762576 | tf_op jit(solution)/shard_map/reduce_scatter | solution.py:198
  2369.9 22.3 all-reduce.7
  2395.2 1335.7 %all-reduce.13.cloned.1.call-done = (f32[384,1536]{1,0:T(8,128)}, f32[384,256]{1,0:T(8,128)}, f32[384,256]{1,0:T(8,128)}, f32[384,1536]{1,0:T(8,128)}, f32[1536,...) async-done(((f32[384,1536]{1,0:T(8,128)}, f32[384,256]{1,0:T(8,128)}, f32[384,256]{1,0:T(8,128)}, f32[384,1536]{1,0:T(8,128)}, f32[1536,2240]{0,1:T(8,128)}, ...) | async-done | bytes 46792720 | tf_op jit(solution)/shard_map/psum | solution.py:261
  (289 shorter events, 292.4 us)
Async XLA Ops:
  7.2 72.3 %all-gather.13.cloned.1.call-start = ((), (), s32[]{:S(2)}) async-start(), calls=%async_computation.10 | async-start | bytes 1179648 | tf_op jit(solution)/shard_map/all_gather | solution.py:170
  39.5 86.0 %copy-start.33 = (f32[128,64]{0,1:T(8,128)}, f32[128,64]{0,1:T(8,128)S(1)}, u32[]{:S(2)}) copy-start(f32[128,64]{0,1:T(8,128)S(1)} %get-tuple-element.287) | copy-start | bytes 98308
  40.2 77.9 %all-gather.15.cloned.1.call-start = ((), (), s32[]{:S(2)}) async-start(), calls=%async_computation.11 | async-start | bytes 5898240 | tf_op jit(solution)/shard_map/all_gather | solution.py:145
  41.0 119.1 %all-gather.11.cloned.1.call-start = ((), (), s32[]{:S(2)}) async-start(), calls=%async_computation.9 | async-start | bytes 1179648 | tf_op jit(solution)/shard_map/all_gather | solution.py:171
  50.7 148.0 %all-gather.17.cloned.1.call-start = ((), (), s32[]{:S(2)}) async-start(), calls=%async_computation.12 | async-start | bytes 5898240 | tf_op jit(solution)/shard_map/all_gather | solution.py:151
  51.2 316.8 %all-gather.19.cloned.1.call-start = ((), (), s32[]{:S(2)}) async-start(), calls=%async_computation.13 | async-start | bytes 34406400 | tf_op jit(solution)/shard_map/all_gather | solution.py:185
  51.8 485.5 %all-gather.21.cloned.1.call-start = ((), (), s32[]{:S(2)}) async-start(), calls=%async_computation.14 | async-start | bytes 34406400 | tf_op jit(solution)/shard_map/all_gather | solution.py:186
  52.4 654.4 %all-gather.23.cloned.1.call-start = ((), (), s32[]{:S(2)}) async-start(), calls=%async_computation.15 | async-start | bytes 34406400 | tf_op jit(solution)/shard_map/all_gather | solution.py:187
  53.2 854.9 %reduce-scatter.10.cloned.1.call-start = ((), (), s32[]{:S(2)}) async-start(), calls=%async_computation.16 | async-start | bytes 2359296 | tf_op jit(solution)/shard_map/reduce_scatter | solution.py:215
  203.9 333.4 %copy-start.11 = (bf16[256,1536]{1,0:T(8,128)(2,1)}, bf16[256,1536]{1,0:T(8,128)(2,1)S(1)}, u32[]{:S(2)}) copy-start(bf16[256,1536]{1,0:T(8,128)(2,1)S(1)} %multiply_convert_fusion.3) | copy-start | bytes 2359300
  387.9 318.9 %copy-start.23 = (bf16[2,128,1536]{2,1,0:T(8,128)(2,1)S(1)}, bf16[2,128,1536]{2,1,0:T(8,128)(2,1)}, u32[]{:S(2)}) copy-start(bf16[2,128,1536]{2,1,0:T(8,128)(2,1)} %param.33) | copy-start | bytes 2359300
  764.7 76.7 %copy-start.41 = (f32[1536]{0:T(1024)S(1)}, f32[1536]{0:T(1024)}, u32[]{:S(2)}) copy-start(f32[1536]{0:T(1024)} %copy-done.40) | copy-start | bytes 18436
  764.7 76.7 %copy-start.48 = (f32[2,128]{1,0:T(2,128)S(1)}, f32[2,128]{1,0:T(2,128)}, u32[]{:S(2)}) copy-start(f32[2,128]{1,0:T(2,128)} %get-tuple-element.283) | copy-start | bytes 3076
  840.5 67.6 %copy-start.34 = (f32[128,64]{0,1:T(8,128)S(1)}, f32[128,64]{0,1:T(8,128)}, u32[]{:S(2)}) copy-start(f32[128,64]{0,1:T(8,128)} %copy-done.33) | copy-start | bytes 98308
  840.6 138.7 %reduce-scatter.12.cloned.1.call-start = ((), (), s32[]{:S(2)}) async-start(), calls=%async_computation.17 | async-start | bytes 2359296 | tf_op jit(solution)/shard_map/reduce_scatter | solution.py:216
  841.3 234.1 %reduce-scatter.16.cloned.1.call-start = ((), (), s32[]{:S(2)}) async-start(), calls=%async_computation.19 | async-start | bytes 1966080 | tf_op jit(solution)/shard_map/reduce_scatter | solution.py:254
  909.3 74.6 %copy-start.32 = (f32[2,128,2,6,128]{1,0,4,3,2:T(2,128)S(1)}, f32[2,128,2,6,128]{1,0,4,3,2:T(2,128)}, u32[]{:S(2)}) copy-start(f32[2,128,2,6,128]{1,0,4,3,2:T(2,128)} %get-tuple-element.118) | copy-start | bytes 4718596
  911.0 164.5 %reduce-scatter.18.cloned.1.call-start = ((), (), s32[]{:S(2)}) async-start(), calls=%async_computation.20 | async-start | bytes 1966080 | tf_op jit(solution)/shard_map/reduce_scatter | solution.py:256
  983.6 139.5 %reduce-scatter.14.cloned.1.call-start = ((), (), s32[]{:S(2)}) async-start(), calls=%async_computation.18 | async-start | bytes 11796480 | tf_op jit(solution)/shard_map/reduce_scatter | solution.py:252
  994.5 210.3 %reduce-scatter.20.cloned.1.call-start = ((), (), s32[]{:S(2)}) async-start(), calls=%async_computation.21 | async-start | bytes 11796480 | tf_op jit(solution)/shard_map/reduce_scatter | solution.py:258
  1001.2 579.9 %reduce-scatter.22.cloned.1.call-start = ((), (), s32[]{:S(2)}) async-start(), calls=%async_computation.22 | async-start | bytes 68812800 | tf_op jit(solution)/shard_map/reduce_scatter | solution.py:194
  1025.4 932.1 %reduce-scatter.24.cloned.1.call-start = ((), (), s32[]{:S(2)}) async-start(), calls=%async_computation.23 | async-start | bytes 68812800 | tf_op jit(solution)/shard_map/reduce_scatter | solution.py:197
  1048.1 1285.8 %reduce-scatter.26.cloned.1.call-start = ((), (), s32[]{:S(2)}) async-start(), calls=%async_computation.24 | async-start | bytes 68812800 | tf_op jit(solution)/shard_map/reduce_scatter | solution.py:198
  1075.3 2655.6 %all-reduce.13.cloned.1.call-start = ((), (), s32[]{:S(2)}) async-start(), calls=%async_computation.25 | async-start | bytes 93585408 | tf_op jit(solution)/shard_map/psum | solution.py:261
  (57 other events, 423.9 us)
Sparse Core Ops, SparseCore 0:
  40.3 39.0 all-gather.12
  81.0 37.0 all-gather.14
  120.8 39.2 all-gather.10
  161.5 37.1 all-gather.16
  200.1 167.8 all-gather.18
  369.4 167.8 all-gather.20
  538.9 167.8 all-gather.22
  840.7 67.3 reduce-scatter.9
  912.2 67.0 reduce-scatter.11
  982.3 27.8 reduce-scatter.15
  1013.5 28.1 reduce-scatter.17
  1044.7 78.3 reduce-scatter.13
  1126.2 78.4 reduce-scatter.19
  1207.2 373.8 reduce-scatter.21
  1583.7 373.8 reduce-scatter.23
  1960.0 373.8 reduce-scatter.25
  2340.6 1390.2 all-reduce.12
where the time goes:
time: 3790 us; the launch traced here: 3780 us
  waiting for transfers between devices  3310 us (87%)
  matrix products  239 us (6%)
  local copies, waits for them, and re-layouts  117 us (3%)
  blocking collectives  72.7 us (2%)
    psum x1, waiting for transfers between devices, shards(): lax.psum((shard_gain_a, shard_query, shard_b_query, shard_key, shard_b_ke...  1340 us
    reduce_scatter x1, waiting for transfers between devices, shards(): lax.psum_scatter(matmul(normed_two, grad_up, 0, 0), 'dp', scatter_dimensi...  377 us
    reduce_scatter x1, waiting for transfers between devices, shards(): lax.psum_scatter(matmul(hidden, grad_top, 0, 0), 'dp', scatter_dimension=...  376 us
    reduce_scatter x1, waiting for transfers between devices, shards(): lax.psum_scatter(matmul(normed_two, grad_gate, 0, 0), 'dp', scatter_dimen...  376 us
    dot_general x21, matrix products, matmul(): lax.dot_general(left, right, (((left_dim,), (right_dim,)), ((), ())), pre...  207 us
    all_gather x1, waiting for transfers between devices, shards(): lax.all_gather(w_gate, 'dp', axis=1, tiled=True)  164 us
    all_gather x1, waiting for transfers between devices, shards(): lax.all_gather(w_down, 'dp', axis=0, tiled=True)  150 us
    all_gather x1, waiting for transfers between devices, shards(): lax.all_gather(w_up, 'dp', axis=1, tiled=True)  149 us
  transfers between devices with their start and end apart: 17, of which 15 were waited for; matrix products, arithmetic and copies ran while one was open for 5% of the time, Pallas kernels for 0%

commit v1 on v0

v1 whole, which is shorter than its diff:
```python
import functools
import math

import jax
import jax.numpy as jnp
from jax import lax
from jax.experimental import pallas as pl
from jax.experimental.pallas import tpu as pltpu
from jax.sharding import PartitionSpec as P

HEADS = 12
KV_HEADS = 2
HEAD = 128
GROUP = HEADS // KV_HEADS

EPSILON = 1e-06
THETA = 1000000.0
BF = jnp.bfloat16
F32 = jnp.float32


def matmul(left, right, left_dim, right_dim):
    return lax.dot_general(
        left, right, (((left_dim,), (right_dim,)), ((), ())), preferred_element_type=F32
    )


def dot_nt(left, right):
    return matmul(left, right, 1, 1)


def dot_tn(left, right):
    return matmul(left, right, 0, 0)


def dot_nn(left, right):
    return matmul(left, right, 1, 0)


def block_positions(block_pair, n_ctx, seq_tok):
    half_blk = seq_tok // 2
    row_ids = jnp.arange(n_ctx * seq_tok, dtype=jnp.int32)
    owner = row_ids // seq_tok
    within = row_ids % seq_tok
    matches = owner[:, None] == jnp.arange(n_ctx, dtype=jnp.int32)[None, :]
    first = jnp.sum(jnp.where(matches, block_pair[None, :], 0), 1)
    chosen = jnp.where(within < half_blk, first, 2 * n_ctx - 1 - first)
    return chosen * half_blk + within % half_blk


def rope_tables(positions):
    half_size = HEAD // 2
    freqs = jnp.exp(jnp.arange(half_size, dtype=F32) * (-math.log(THETA) / half_size))
    angle = positions.astype(F32)[:, None] * freqs[None, :]
    cosine, sine = jnp.cos(angle), jnp.sin(angle)
    return jnp.concatenate([cosine, cosine, -sine, sine], 1)


def call(kernel, name, args, specs, outs, out_specs=None, grid=(), flops=0, exps=0, scratch=()):
    size = sum(math.prod(a.shape) * a.dtype.itemsize for a in list(args) + list(outs))
    if out_specs is None:
        out_specs = [whole(o) for o in outs]
    return pl.pallas_call(
        kernel,
        grid=grid,
        in_specs=specs,
        out_specs=out_specs,
        out_shape=outs,
        scratch_shapes=scratch,
        cost_estimate=pl.CostEstimate(flops=flops, transcendentals=exps, bytes_accessed=size),
        name=name,
    )(*args)


SCALARS = pl.BlockSpec(memory_space=pltpu.SMEM)


def whole(array):
    zeros = (0,) * len(array.shape)
    return pl.BlockSpec(array.shape, lambda *_: zeros)


def fixed(array):
    zeros = (0,) * len(array.shape)
    return pl.BlockSpec(array.shape, lambda *_: zeros, pipeline_mode=pl.Buffered(1))


def shape(dims, dtype):
    return jax.ShapeDtypeStruct(tuple(dims), dtype)


def lanes(ref, start, size):
    return ref.at[:, pl.ds(pl.multiple_of(start * size, 128), size)]


def scale_of(x):
    return lax.rsqrt(jnp.mean(x * x, -1, keepdims=True) + EPSILON)


def turn(x, table, sign):
    tables = jnp.concatenate([table] * (x.shape[0] // table.shape[0]), 0)
    return x * tables[:, :HEAD] + sign * (pltpu.roll(x, HEAD // 2, 1) * tables[:, HEAD:])


def norm_kv_kernel(n, seq, at, tok, gain, bias, table, *refs):
    weights, (normed, kv) = refs[:n], refs[n:]
    x = tok[...].astype(F32)
    normed[...] = (x * scale_of(x) * gain[...]).astype(BF)
    part = weights[0].shape[0]
    acc = bias[...]
    for p in range(n):
        acc = acc + dot_nn(lanes(normed, at[2 + p], part)[...], weights[p][...])
    toks = x.shape[0] // seq
    for k in range(KV_HEADS):
        key = turn(acc[:, k * HEAD : (k + 1) * HEAD], table[...], 1.0).astype(BF)
        value = acc[:, (KV_HEADS + k) * HEAD : (KV_HEADS + k + 1) * HEAD].astype(BF)
        for s in range(seq):
            kv[s, k, :, :HEAD] = key[s * toks : (s + 1) * toks]
            kv[s, k, :, HEAD:] = value[s * toks : (s + 1) * toks]


def query_kernel(n, at, normed, bias, table, *refs):
    weights, (out,) = refs[:n], refs[n:]
    part = weights[0].shape[0]
    acc = bias[...]
    for p in range(n):
        acc = acc + dot_nn(lanes(normed, at[2 + p], part)[...], weights[p][...])
    for h in range(HEADS):
        cols = slice(h * HEAD, (h + 1) * HEAD)
        out[:, cols] = turn(acc[:, cols], table[...], 1.0).astype(BF)


def stack_heads(ref):
    return jnp.concatenate([ref[:, g * HEAD : (g + 1) * HEAD] for g in range(GROUP)], 0)


def softmax_of(q, k, qpos, kpos):
    scores = dot_nt(q, k) * (HEAD**-0.5)
    allowed = kpos <= jnp.concatenate([qpos] * GROUP, 0)
    scores = jnp.where(allowed, scores, -jnp.inf)
    expon = jnp.exp(scores - jnp.max(scores, -1, keepdims=True))
    return expon / jnp.sum(expon, -1, keepdims=True)


def attend_forward_kernel(q_ref, kv_ref, qpos, kpos, out_ref):
    rows = q_ref.shape[0]
    keys = kv_ref.shape[0] * kv_ref.shape[1]
    k = kv_ref[:, :, :HEAD].reshape(keys, HEAD)
    v = kv_ref[:, :, HEAD:].reshape(keys, HEAD)
    probs = softmax_of(stack_heads(q_ref), k, qpos[...], kpos[...]).astype(BF)
    mixed = dot_nn(probs, v).astype(BF)
    for g in range(GROUP):
        out_ref[:, g * HEAD : (g + 1) * HEAD] = mixed[g * rows : (g + 1) * rows]


def attention_specs(kv_all):
    n_ctx, _, _, seq_tok, _ = kv_all.shape
    rows = pl.BlockSpec((seq_tok, GROUP * HEAD), lambda s, k: (s, k))
    kv = pl.BlockSpec((n_ctx, None, None, seq_tok, 2 * HEAD), lambda s, k: (0, s, k, 0, 0))
    return rows, kv


def attend_forward(queries, kv_all, qpos, kpos):
    rows, kv = attention_specs(kv_all)
    keys = kv_all.shape[0] * kv_all.shape[3]
    return call(
        attend_forward_kernel,
        "attend_forward",
        (queries, kv_all, qpos, kpos),
        [rows, kv, whole(qpos), whole(kpos)],
        [shape(queries.shape, BF)],
        [rows],
        (kv_all.shape[1], KV_HEADS),
        4 * queries.size * keys,
        queries.shape[0] * HEADS * keys,
    )[0]


def attend_backward_kernel(q_ref, kv_ref, go_ref, qpos, kpos, table, gq_ref, gkv_ref):
    rows = q_ref.shape[0]
    n_ctx, seq_tok, _ = kv_ref.shape
    keys = n_ctx * seq_tok
    scale = HEAD**-0.5
    k = kv_ref[:, :, :HEAD].reshape(keys, HEAD)
    v = kv_ref[:, :, HEAD:].reshape(keys, HEAD)
    q = stack_heads(q_ref)
    go = stack_heads(go_ref)
    probs = softmax_of(q, k, qpos[...], kpos[...])
    gkv_ref[:, :, HEAD:] = dot_tn(probs.astype(BF), go).astype(BF).reshape(n_ctx, seq_tok, HEAD)
    grad_probs = dot_nt(go, v)
    centre = jnp.sum(probs * grad_probs, -1, keepdims=True)
    grad_scores = (probs * (grad_probs - centre)).astype(BF)
    gq = turn(dot_nn(grad_scores, k) * scale, table[...], -1.0).astype(BF)
    for g in range(GROUP):
        gq_ref[:, g * HEAD : (g + 1) * HEAD] = gq[g * rows : (g + 1) * rows]
    gk = dot_tn(grad_scores, q) * scale
    gkv_ref[:, :, :HEAD] = gk.astype(BF).reshape(n_ctx, seq_tok, HEAD)


def attend_backward(queries, kv_all, grad_mixed, qpos, kpos, table):
    rows, kv = attention_specs(kv_all)
    keys = kv_all.shape[0] * kv_all.shape[3]
    return call(
        attend_backward_kernel,
        "attend_backward",
        (queries, kv_all, grad_mixed, qpos, kpos, table),
        [rows, kv, rows, whole(qpos), whole(kpos), whole(table)],
        [shape(queries.shape, BF), shape(kv_all.shape, BF)],
        [rows, kv],
        (kv_all.shape[1], KV_HEADS),
        10 * queries.size * keys,
        queries.shape[0] * HEADS * keys,
    )


def out_norm_kernel(n, at, tok, attn, gain, *refs):
    weights, (middle, normed) = refs[:n], refs[n:]
    part = weights[0].shape[0]
    acc = tok[...].astype(F32)
    for p in range(n):
        acc = acc + dot_nn(lanes(attn, at[2 + p], part)[...], weights[p][...])
    middle[...] = acc
    normed[...] = (acc * scale_of(acc) * gain[...]).astype(BF)


def hidden_back_kernel(n, wd, *refs):
    rows, out = refs[:n], refs[n]
    step = rows[0].shape[0]
    for p in range(n):
        out[:, p * step : (p + 1) * step] = dot_nt(wd[...], rows[p][...]).astype(BF)


def unit_tile(total):
    return max(t for t in range(16, 513, 16) if total % t == 0)


def hidden_back(w_down, blocks):
    n = len(blocks)
    rows, width = blocks[0].shape
    wide = w_down.shape[0]
    tile = unit_tile(wide)
    return call(
        functools.partial(hidden_back_kernel, n),
        "hidden_back",
        (w_down, *blocks),
        [pl.BlockSpec((tile, width), lambda i: (i, 0))] + [fixed(b) for b in blocks],
        [shape((wide, n * rows), BF)],
        [pl.BlockSpec((tile, n * rows), lambda i: (i, 0))],
        (wide // tile,),
        2 * n * rows * width * wide,
    )[0]


def units_kernel(n, gh, wg, wu, *refs):
    rows, (hidden, gg, gu) = refs[:n], refs[n:]
    step = rows[0].shape[0]
    for p in range(n):
        cols = slice(p * step, (p + 1) * step)
        gate = dot_nt(wg[...], rows[p][...])
        up = dot_nt(wu[...], rows[p][...])
        grad = gh[:, cols].astype(F32)
        sigma = 1.0 / (1.0 + jnp.exp(-gate))
        act = gate * sigma
        hidden[:, cols] = (act * up).astype(BF)
        gu[:, cols] = (grad * act).astype(BF)
        gg[:, cols] = (grad * up * sigma * (1.0 + gate - act)).astype(BF)


def units(grad_hidden, first, w_gate, w_up, blocks):
    n = len(blocks)
    rows, width = blocks[0].shape
    wide = w_gate.shape[0]
    tile = unit_tile(wide)
    weight = pl.BlockSpec((tile, width), lambda i: (i, 0))
    out = pl.BlockSpec((tile, n * rows), lambda i: (i, 0))
    return call(
        functools.partial(units_kernel, n),
        "units",
        (grad_hidden, w_gate, w_up, *blocks),
        [pl.BlockSpec((tile, n * rows), lambda i: (i, first)), weight, weight]
        + [fixed(b) for b in blocks],
        [shape((wide, n * rows), BF)] * 3,
        [out] * 3,
        (wide // tile,),
        4 * n * rows * width * wide,
        n * rows * wide,
    )


def weight_cols_kernel(n, tiles, at, own, near, *refs):
    xs, outs, x = refs[:n], refs[n : n + tiles], refs[n + tiles]
    rows = xs[0].shape[0]
    half = x.shape[1]

    @pl.when(pl.program_id(0) == 0)
    def _():
        for p in range(n):
            x[p * rows : (p + 1) * rows, :] = lanes(xs[p], at[0], half)[...]

    mid = own.shape[1]
    total = dot_nn(own[...], x[:mid, :]) + dot_nn(near[...], x[mid:, :])
    tile = half // tiles
    for i in range(tiles):
        outs[i][...] = total[:, i * tile : (i + 1) * tile].astype(BF)


def weight_cols(at, xs, own, near, tiles):
    n = len(xs)
    rows, width = xs[0].shape
    half = width // 2
    wide, cols = own.shape
    tile = unit_tile(wide)
    part = pl.BlockSpec((tile, cols), lambda i: (i, 0))
    return call(
        functools.partial(weight_cols_kernel, n, tiles),
        "weight_cols",
        (at, own, near, *xs),
        [SCALARS, part, part] + [fixed(a) for a in xs],
        [shape((wide, half // tiles), BF)] * tiles,
        [pl.BlockSpec((tile, half // tiles), lambda i: (i, 0))] * tiles,
        (wide // tile,),
        2 * n * rows * half * wide,
        scratch=[pltpu.VMEM((n * rows, half), BF)],
    )


def middle_back_kernel(n, at, grad, middle, top, gain, *refs):
    weights, (gm_ref, gb_ref, ga_ref, dg_ref) = refs[:n], refs[n:]
    part = weights[0].shape[0]
    v, dy = middle[...], grad[...]
    scale = scale_of(v)
    dg_ref[...] = jnp.sum(dy * v * scale, 0, keepdims=True)
    a = dy * gain[...]
    gm = top[...].astype(F32) + scale * a - v * (scale**3 * jnp.mean(a * v, -1, keepdims=True))
    gm_ref[...] = gm
    gb = gm.astype(BF)
    gb_ref[...] = gb
    for p in range(n):
        lanes(ga_ref, at[2 + p], part)[...] = dot_nt(gb, weights[p][...]).astype(BF)


def grad_kv_kernel(recv, table, out):
    n_ctx, seq, _, toks, _ = recv.shape
    for k in range(KV_HEADS):
        for s in range(seq):
            total = recv[0, s, k].astype(F32)
            for c in range(1, n_ctx):
                total = total + recv[c, s, k].astype(F32)
            at = slice(s * toks, (s + 1) * toks)
            out[at, k * HEAD : (k + 1) * HEAD] = turn(total[:, :HEAD], table[...], -1.0).astype(BF)
            out[at, (KV_HEADS + k) * HEAD : (KV_HEADS + k + 1) * HEAD] = total[:, HEAD:].astype(BF)


def input_back_kernel(n, at, gq, gkv, tok, gain, gm, *refs):
    wq, wkv, (gi_ref, dg_ref, db_ref, dy_ref) = refs[:n], refs[n : 2 * n], refs[2 * n :]
    part = wq[0].shape[0]
    width = gq.shape[1]
    for p in range(n):
        lanes(dy_ref, at[2 + p], part)[...] = dot_nt(gq[...], wq[p][...]) + dot_nt(
            gkv[...], wkv[p][...]
        )
    db_ref[:, :width] = jnp.sum(gq[...].astype(F32), 0, keepdims=True)
    db_ref[:, width:] = jnp.sum(gkv[...].astype(F32), 0, keepdims=True)
    v, dy = tok[...].astype(F32), dy_ref[...]
    scale = scale_of(v)
    dg_ref[...] = jnp.sum(dy * v * scale, 0, keepdims=True)
    a = dy * gain[...]
    gi_ref[...] = gm[...] + scale * a - v * (scale**3 * jnp.mean(a * v, -1, keepdims=True))


def split_weight_kernel(n, at, *refs):
    xs, gs, (keep, send) = refs[:n], refs[n : 2 * n], refs[2 * n :]
    half = keep.shape[1]
    for out, which in ((keep, at[0]), (send, 1 - at[0])):
        total = dot_tn(xs[0][...], lanes(gs[0], which, half)[...])
        for p in range(1, n):
            total = total + dot_tn(xs[p][...], lanes(gs[p], which, half)[...])
        out[...] = total.astype(out.dtype)


def split_weight(at, xs, gs):
    part, wide = xs[0].shape[1], gs[0].shape[1]
    args = (at, *xs, *gs)
    return call(
        functools.partial(split_weight_kernel, len(xs)),
        "split_weight",
        args,
        [SCALARS] + [whole(a) for a in args[1:]],
        [shape((part, wide // 2), F32), shape((part, wide // 2), BF)],
        flops=2 * len(xs) * xs[0].shape[0] * part * wide,
    )


def join_kernel(tiles, at, *refs):
    mine, theirs, out = refs[:tiles], refs[tiles : 2 * tiles], refs[2 * tiles]
    tile = mine[0].shape[1]
    for j in range(2 * tiles):
        for side, ref in ((0, mine), (1, theirs)):

            @pl.when((at[0] ^ side) == j // tiles)
            def _():
                out[:, j * tile : (j + 1) * tile] = ref[j % tiles][...].astype(F32)


def join(at, mine, theirs):
    tiles = len(mine)
    wide, cols = mine[0].shape
    tile = unit_tile(wide)
    part = pl.BlockSpec((tile, cols), lambda i: (i, 0))
    return call(
        functools.partial(join_kernel, tiles),
        "join",
        (at, *mine, *theirs),
        [SCALARS] + [part] * (2 * tiles),
        [shape((wide, 2 * tiles * cols), F32)],
        [pl.BlockSpec((tile, 2 * tiles * cols), lambda i: (i, 0))],
        (wide // tile,),
    )[0]


def swap(value, axis, offset):
    size = lax.axis_size(axis)
    return lax.ppermute(value, axis, [(i, i ^ offset) for i in range(size)])


def offsets_of(size):
    order = [0]
    step = size // 2
    while step:
        order += [o ^ step for o in order]
        step //= 2
    return order


def gather_dp(value):
    blocks = [value]
    step = lax.axis_size("dp") // 2
    while step:
        blocks += [swap(b, "dp", step) for b in blocks]
        step //= 2
    return blocks


def exchange_dp(value, part):
    here = lax.axis_index("dp")
    out = [lax.dynamic_slice_in_dim(value, here * part, part, 1)]
    for offset in offsets_of(lax.axis_size("dp"))[1:]:
        theirs = lax.dynamic_slice_in_dim(value, (here ^ offset) * part, part, 1)
        out.append(swap(theirs, "dp", offset))
    return out


def scatter_dp(value):
    size = lax.axis_size("dp")
    step = 1
    while step < size:
        half = value.shape[0] // 2
        value = value[:half].astype(F32) + swap(value[half:].astype(BF), "dp", step).astype(F32)
        step *= 2
    return value


def ctx_sums(blocks):
    length = lax.axis_size("ctx") // 2
    last = length - 1
    place = lax.axis_index("ctx") // 2
    depth = length // 2 - 1

    def send(value, pairs):
        return lax.ppermute(
            value, "ctx", [(2 * i + y, 2 * j + y) for i, j in pairs for y in range(2)]
        )

    n = len(blocks)
    state = list(blocks)
    other = [None] * n
    before = []
    n_stage = 2 * depth + 2
    for slot in range(n + n_stage - 1):
        moves = []
        for j in range(depth):
            going, coming = slot - j, slot - (2 * depth - j)
            has_in, has_out = 0 <= going < n, 0 <= coming < n
            inward = [(j, j + 1), (last - j, last - j - 1)]
            outward = [(b, a) for a, b in inward]
            outer = (place == j) | (place == last - j)
            if has_in and has_out and state[going].shape == state[coming].shape:
                value = jnp.where(outer, state[going], state[coming])
                moves.append((value, inward + outward, going, coming, outer))
                continue
            if has_in:
                moves.append((state[going], inward, going, None, outer))
            if has_out:
                moves.append((state[coming], outward, None, coming, outer))
        if 0 <= slot - depth < n:
            b = slot - depth
            moves.append((state[b], [(depth, depth + 1), (depth + 1, depth)], b, None, None))
        if 0 <= slot - n_stage + 1 < n:
            moves.append((state[slot - n_stage + 1], None, None, None, None))
        sent, _ = lax.optimization_barrier(([m[0] for m in moves], before))
        before = []
        for value, (_, pairs, going, coming, outer) in zip(sent, moves):
            got = swap(value, "ctx", 1) if pairs is None else send(value, pairs)
            before.append(got)
            if pairs is None:
                other[slot - n_stage + 1] = got
            if going is not None:
                state[going] = (state[going].astype(F32) + got.astype(F32)).astype(BF)
            if coming is not None:
                state[coming] = jnp.where(outer, got, state[coming])
    return state, other


def shards(
    tokens,
    block_pair,
    gain_attn,
    w_query,
    b_query,
    w_key,
    b_key,
    w_value,
    b_value,
    w_out,
    gain_mlp,
    w_gate,
    w_up,
    w_down,
    cotangent,
):
    n_ctx = lax.axis_size("ctx")
    n_dp = lax.axis_size("dp")
    dp_index = lax.axis_index("dp")
    parity = lax.axis_index("ctx") % 2
    seq_grp, seq_tok, width = tokens.shape
    kv_width = KV_HEADS * HEAD
    rows = seq_grp * seq_tok
    part = w_query.shape[0]
    key_pos = block_positions(block_pair, n_ctx, seq_tok)
    query_pos = lax.dynamic_slice_in_dim(key_pos, lax.axis_index("ctx") * seq_tok, seq_tok)
    table = rope_tables(query_pos)
    qpos = query_pos[:, None]
    kpos = key_pos[None, :]
    at = jnp.stack([parity, dp_index] + [dp_index ^ o for o in offsets_of(n_dp)]).astype(jnp.int32)

    small = lax.all_gather(
        jnp.concatenate([gain_attn, gain_mlp, b_query, b_key, b_value])[None], "dp", axis=0, tiled=True
    )
    cuts = [0]
    for item in (gain_attn, gain_mlp, b_query, b_key, b_value):
        cuts.append(cuts[-1] + item.shape[0])
    gain_one, gain_two, bias_query, bias_key, bias_value = [
        small[:, a:b].reshape(1, -1).astype(F32) for a, b in zip(cuts[:-1], cuts[1:])
    ]
    bias_kv = jnp.concatenate([bias_key, bias_value], 1)
    full_kv = gather_dp(jnp.concatenate([w_key, w_value], 1))
    full_query = gather_dp(w_query)
    full_out = gather_dp(w_out)

    inputs = tokens.reshape(rows, width)
    args = (at, inputs, gain_one, bias_kv, table, *full_kv)
    normed_one, kv_own = call(
        functools.partial(norm_kv_kernel, n_dp, seq_grp),
        "norm_kv",
        args,
        [SCALARS] + [whole(a) for a in args[1:]],
        [shape((rows, width), BF), shape((seq_grp, KV_HEADS, seq_tok, 2 * HEAD), BF)],
        flops=4 * rows * width * kv_width,
    )
    kv_all = lax.all_gather(kv_own, "ctx", axis=0, tiled=False)
    args = (at, normed_one, bias_query, table, *full_query)
    queries = call(
        functools.partial(query_kernel, n_dp),
        "query",
        args,
        [SCALARS] + [whole(a) for a in args[1:]],
        [shape((rows, width), BF)],
        flops=2 * rows * width * width,
    )[0]
    attn_vec = attend_forward(queries, kv_all, qpos, kpos)
    args = (at, inputs, attn_vec, gain_two, *full_out)
    middle, normed_two = call(
        functools.partial(out_norm_kernel, n_dp),
        "out_norm",
        args,
        [SCALARS] + [whole(a) for a in args[1:]],
        [shape((rows, width), F32), shape((rows, width), BF)],
        flops=2 * rows * width * width,
    )

    grad_rows = cotangent.reshape(rows, width)
    top_own, top_near = gather_dp(grad_rows), gather_dp(swap(grad_rows, "ctx", 1))
    norm_own, norm_near = gather_dp(normed_two), gather_dp(swap(normed_two, "ctx", 1))
    wide_gate, wide_up = w_gate.T, w_up.T
    grad_hidden = hidden_back(w_down, top_own + top_near)
    hidden, grad_gate, grad_up = units(grad_hidden, 0, wide_gate, wide_up, norm_own)
    near = units(grad_hidden, 1, wide_gate, wide_up, norm_near)
    tiles = 3
    part_down = weight_cols(at, top_own + top_near, hidden, near[0], tiles)
    part_gate = weight_cols(at, norm_own + norm_near, grad_gate, near[1], tiles)
    part_up = weight_cols(at, norm_own + norm_near, grad_up, near[2], tiles)

    grad_norm_two = scatter_dp(
        (matmul(grad_gate, wide_gate, 0, 0) + matmul(grad_up, wide_up, 0, 0)).astype(BF)
    )
    mlp_out = scatter_dp(matmul(hidden, w_down, 0, 0).astype(BF))
    layer_out = (middle + mlp_out).astype(BF).reshape(tokens.shape)

    args = (at, grad_norm_two, middle, grad_rows, gain_two, *full_out)
    grad_middle, grad_branch, grad_attn, grad_gain_m = call(
        functools.partial(middle_back_kernel, n_dp),
        "middle_back",
        args,
        [SCALARS] + [whole(a) for a in args[1:]],
        [
            shape((rows, width), F32),
            shape((rows, width), BF),
            shape((rows, width), BF),
            shape((1, width), F32),
        ],
        flops=2 * rows * width * width,
    )
    grad_query, grad_kv_all = attend_backward(queries, kv_all, grad_attn, qpos, kpos, table)
    recv = lax.all_to_all(grad_kv_all, "ctx", 0, 0, tiled=True)
    grad_kv = call(
        grad_kv_kernel,
        "grad_kv",
        (recv, table),
        [whole(recv), whole(table)],
        [shape((rows, 2 * kv_width), BF)],
    )[0]
    args = (at, grad_query, grad_kv, inputs, gain_one, grad_middle, *full_query, *full_kv)
    grad_input, grad_gain_a, grad_bias = call(
        functools.partial(input_back_kernel, n_dp),
        "input_back",
        args,
        [SCALARS] + [whole(a) for a in args[1:]],
        [shape((rows, width), F32), shape((1, width), F32), shape((1, width + 2 * kv_width), F32)],
        flops=2 * rows * width * (width + 2 * kv_width),
        scratch=[pltpu.VMEM((rows, width), F32)],
    )

    normed_cols = exchange_dp(normed_one, part)
    attn_cols = exchange_dp(attn_vec, part)
    halves = [
        split_weight(at, attn_cols, gather_dp(grad_branch)),
        split_weight(at, normed_cols, gather_dp(grad_query)),
        split_weight(at, normed_cols, gather_dp(grad_kv)),
    ]
    paired = [(keep + swap(send, "ctx", 1).astype(F32)).astype(BF) for keep, send in halves]

    own, other = ctx_sums(list(part_down) + list(part_gate) + list(part_up) + paired)
    grad_w_down = join(at, own[:tiles], other[:tiles])
    grad_w_gate = join(at, own[tiles : 2 * tiles], other[tiles : 2 * tiles]).T
    grad_w_up = join(at, own[2 * tiles : 3 * tiles], other[2 * tiles : 3 * tiles]).T

    def joined(index):
        mine, theirs = own[index].astype(F32), other[index].astype(F32)
        low = jnp.where(parity == 0, mine, theirs)
        high = jnp.where(parity == 0, theirs, mine)
        return jnp.concatenate([low, high], 1)

    grad_w_out, grad_w_query, grad_w_kv = [joined(3 * tiles + i) for i in range(3)]

    vectors = [
        v.reshape(n_dp, -1)
        for v in (
            grad_gain_a,
            grad_gain_m,
            grad_bias[:, :width],
            grad_bias[:, width : width + kv_width],
            grad_bias[:, width + kv_width :],
        )
    ]
    vectors = jnp.concatenate(vectors, 1)
    order = [lax.dynamic_slice_in_dim(vectors, at[2 + p], 1, 0) for p in range(n_dp)]
    step = 1
    while step < n_dp:
        keep, send = order[: len(order) // 2], order[len(order) // 2 :]
        got = swap(jnp.concatenate(send, 0), "dp", step)
        order = [k + got[i : i + 1] for i, k in enumerate(keep)]
        step *= 2
    share = order[0]
    step = 1
    while step < n_ctx:
        share = share + swap(share, "ctx", step)
        step *= 2
    shares = [share[0, a:b] for a, b in zip(cuts[:-1], cuts[1:])]
    return (
        layer_out,
        grad_input.reshape(tokens.shape),
        shares[0],
        grad_w_query,
        shares[2],
        grad_w_kv[:, :kv_width],
        shares[3],
        grad_w_kv[:, kv_width:],
        shares[4],
        grad_w_out,
        shares[1],
        grad_w_gate,
        grad_w_up,
        grad_w_down,
    )


def solution(mesh):
    placed = (
        P("dp", "ctx", None),
        P(),
        P("dp"),
        P("dp", None),
        P("dp"),
        P("dp", None),
        P("dp"),
        P("dp", None),
        P("dp"),
        P("dp", None),
        P("dp"),
        P(None, "dp"),
        P(None, "dp"),
        P("dp", None),
        P("dp", "ctx", None),
    )
    return jax.shard_map(
        shards,
        mesh=mesh,
        in_specs=placed,
        out_specs=(
            P("dp", "ctx", None),
            P("dp", "ctx", None),
            P("dp"),
            P("dp", None),
            P("dp"),
            P("dp", None),
            P("dp"),
            P("dp", None),
            P("dp"),
            P("dp", None),
            P("dp"),
            P(None, "dp"),
            P(None, "dp"),
            P("dp", None),
        ),
        check_vma=False,
    )
```

time: 3790 us -> 900 us (0.24)
  waiting for transfers between devices: 3310 us -> 431 us
  matrix products: 239 us -> 31.7 us
  Pallas kernels: 0 us -> 199 us
  starting transfers between devices: 1.15 us -> 111 us
  local copies, waits for them, and re-layouts: 117 us -> 30.3 us
  blocking collectives: 72.7 us -> 6.84 us
  other arithmetic: 25.9 us -> 67.7 us
    reduce_scatter x9 -> x0, waiting for transfers between devices: 1390 us -> none  [the longest x1 377 us: shards(): lax.psum_scatter(matmul(normed_two, grad_up, 0, 0), 'dp', scatter_dimensi...]
    psum x1 -> x0, waiting for transfers between devices: 1340 us -> none  [shards(): lax.psum((shard_gain_a, shard_query, shard_b_query, shard_key, shard_b_ke...]
    all_gather x7 -> x1, waiting for transfers between devices: 573 us -> 0.01 us  [shards(): kv_all = lax.all_gather(kv_own, 'ctx', axis=0, tiled=False)]
    ppermute x0 -> x91, waiting for transfers between devices: none -> 431 us  [the longest x29 250 us: send(): lax.ppermute(value, 'ctx', [(2 * i + y, 2 * j + y) for i, j in pairs for...]
    pallas_call x0 -> x20, Pallas kernels: none -> 199 us  [call(): pl.pallas_call(kernel, grid=grid, in_specs=specs, out_specs=out_specs, ou...]
    dot_general x21 -> x3, matrix products: 207 us -> 31.7 us  [matmul(): lax.dot_general(left, right, (((left_dim,), (right_dim,)), ((), ())), pre...]
    ppermute x0 -> x91, starting transfers between devices: none -> 105 us  [the longest x29 62.9 us: send(): lax.ppermute(value, 'ctx', [(2 * i + y, 2 * j + y) for i, j in pairs for...]
    dynamic_update_slice x2 -> x0, local copies, waits for them, and re-layouts: 40.7 us -> none  [shards(): mixed, log_sum = lax.map(forward_one, (grouped, keys_all, values_all))]
  transfers between devices with their start and end apart: 17 -> 93, of which waited for: 15 -> 35; matrix products, arithmetic and copies ran while one was open for 5% -> 12% of each run, Pallas kernels for 0% -> 18%
where the time goes in v1:
time: 900 us; the launch traced here: 893 us
  waiting for transfers between devices  431 us (48%)
  Pallas kernels  199 us (22%)
  starting transfers between devices  111 us (12%)
  other arithmetic  67.7 us (8%)
  matrix products  31.7 us (4%)
  local copies, waits for them, and re-layouts  30.3 us (3%)
  between operations  15.4 us (2%)
    ppermute x29, waiting for transfers between devices, send(): lax.ppermute(value, 'ctx', [(2 * i + y, 2 * j + y) for i, j in pairs for...  250 us
    pallas_call x20, Pallas kernels, call(): pl.pallas_call(kernel, grid=grid, in_specs=specs, out_specs=out_specs, ou...  199 us
    ppermute x62, waiting for transfers between devices, swap(): return lax.ppermute(value, axis, [(i, i ^ offset) for i in range(size)])  181 us
    ppermute x29, starting transfers between devices, send(): lax.ppermute(value, 'ctx', [(2 * i + y, 2 * j + y) for i, j in pairs for...  62.9 us
    ppermute x62, starting transfers between devices, swap(): return lax.ppermute(value, axis, [(i, i ^ offset) for i in range(size)])  41.9 us
    dot_general x3, matrix products, matmul(): lax.dot_general(left, right, (((left_dim,), (right_dim,)), ((), ())), pre...  31.7 us
    convert_element_type x17, other arithmetic, ctx_sums(): state[going] = (state[going].astype(F32) + got.astype(F32)).astype(BF)  21.7 us
  transfers between devices with their start and end apart: 93, of which 35 were waited for; matrix products, arithmetic and copies ran while one was open for 12% of the time, Pallas kernels for 18%

profile of v1, /device:TPU:8, one launch (start us, length us, event | category | flops | bytes accessed | tf_op | source)
XLA Modules:
  0.0 893.2 jit_solution(3301633950779878796)
XLA Ops:
  35.7 23.9 %collective-permute-done.3.refs_1_ = bf16[384,1536]{1,0:T(8,128)(2,1)} collective-permute-done((bf16[384,1536]{1,0:T(8,128)(2,1)S(1)}, bf16[384,1536]{1,0:T(8,128)(2,1)}, u32[]{:S(2)}, u32[]{:S(2)}) %collective-permute-start.3) | collective-permute-done | bytes 1179680 | tf_op jit(solution)/shard_map/ppermute | solution.py:423
  59.6 41.3 %collective-permute-done.9.refs_1_ = bf16[256,1536]{1,0:T(8,128)(2,1)S(1)} collective-permute-done((bf16[256,1536]{1,0:T(8,128)(2,1)}, bf16[256,1536]{1,0:T(8,128)(2,1)S(1)}, u32[]{:S(2)}, u32[]{:S(2)}) %collective-permute-start.9) | collective-permute-done | bytes 786464 | tf_op jit(solution)/shard_map/ppermute | solution.py:423
  133.1 17.4 %collective-permute-done.16.refs_1_ = bf16[256,1536]{1,0:T(8,128)(2,1)S(1)} collective-permute-done((bf16[256,1536]{1,0:T(8,128)(2,1)}, bf16[256,1536]{1,0:T(8,128)(2,1)S(1)}, u32[]{:S(2)}, u32[]{:S(2)}) %collective-permute-start.16) | collective-permute-done | bytes 786464 | tf_op jit(solution)/shard_map/ppermute | solution.py:423
  152.2 19.8 %hidden_back.1.gh = bf16[2240,2048]{1,0:T(8,128)(2,1)} custom-call(bf16[2240,1536]{1,0:T(8,128)(2,1)} %wd.1, bf16[256,1536]{1,0:T(8,128)(2,1)} %bitcast.50, bf16[256,1536]{1,0:T(8,128)(2,1)} %copy-done.57, bf16[256,1536]{1,0:T(8,128)(2,1)} %collective-permute-done.10.refs_2_, bf16[256,1536]{1,0:T(8,128)(2,1)} %collective-permute-done.11.refs_3_, ...), custom_call_target="tpu_custom_call" | custom-call | flops 14092861440 | bytes 22347776 | tf_op jit(solution)/shard_map/hidden_back/pallas_call | solution.py:63
  173.7 22.0 %units.2 = (bf16[2240,1024]{1,0:T(8,128)(2,1)}, bf16[2240,1024]{1,0:T(8,128)(2,1)}, bf16[2240,1024]{1,0:T(8,128)(2,1)}) custom-call(bf16[2240,2048]{1,0:T(8,128)(2,1)} %hidden_back.1.gh, bf16[2240,1536]{1,0:T(8,128)(2,1)} %bitcast.64, bf16[2240,1536]{1,0:T(8,128)(2,1)} %bitcast.62, bf16[256,1536]{1,0:T(8,128)(2,1)} %get-tuple-element.91.refs_0_, ...), custom_call_target="tpu_custom_call" | custom-call | flops 14092861440 | bytes 39845888 | tf_op jit(solution)/shard_map/units/pallas_call | solution.py:63
  195.7 22.0 %units.3 = (bf16[2240,1024]{1,0:T(8,128)(2,1)}, bf16[2240,1024]{1,0:T(8,128)(2,1)}, bf16[2240,1024]{1,0:T(8,128)(2,1)}) custom-call(bf16[2240,2048]{1,0:T(8,128)(2,1)} %hidden_back.1.gh, bf16[2240,1536]{1,0:T(8,128)(2,1)} %bitcast.65, bf16[2240,1536]{1,0:T(8,128)(2,1)} %bitcast.63, bf16[256,1536]{1,0:T(8,128)(2,1)} %copy-done.54, ...), custom_call_target="tpu_custom_call" | custom-call | flops 14092861440 | bytes 39845888 | tf_op jit(solution)/shard_map/units/pallas_call | solution.py:63
  217.8 12.9 %weight_cols.5 = (bf16[2240,256]{1,0:T(8,128)(2,1)}, bf16[2240,256]{1,0:T(8,128)(2,1)}, bf16[2240,256]{1,0:T(8,128)(2,1)}) custom-call(s32[6]{0:T(128)} %stack.24.at, bf16[2240,1024]{1,0:T(8,128)(2,1)} %get-tuple-element.92.own, bf16[2240,1024]{1,0:T(8,128)(2,1)} %get-tuple-element.110.near, bf16[256,1536]{1,0:T(8,128)(2,1)} %bitcast.51, ...), custom_call_target="tpu_custom_call" | custom-call | flops 7046430720 | bytes 18907160 | tf_op jit(solution)/shard_map/weight_cols/pallas_call | solution.py:63
  232.1 28.1 %collective-permute-done.39 = bf16[2240,256]{1,0:T(8,128)(2,1)S(1)} collective-permute-done((bf16[2240,256]{1,0:T(8,128)(2,1)}, bf16[2240,256]{1,0:T(8,128)(2,1)S(1)}, u32[]{:S(2)}, u32[]{:S(2)}) %collective-permute-start.39) | collective-permute-done | bytes 1146912 | tf_op jit(solution)/shard_map/ppermute | solution.py:470
  266.6 23.6 %collective-permute-done.41 = bf16[2240,256]{1,0:T(8,128)(2,1)} collective-permute-done((bf16[2240,256]{1,0:T(8,128)(2,1)S(1)}, bf16[2240,256]{1,0:T(8,128)(2,1)}, u32[]{:S(2)}, u32[]{:S(2)}) %collective-permute-start.41) | collective-permute-done | bytes 1146912 | tf_op jit(solution)/shard_map/ppermute | solution.py:470
  293.6 12.5 %weight_cols.4 = (bf16[2240,256]{1,0:T(8,128)(2,1)}, bf16[2240,256]{1,0:T(8,128)(2,1)}, bf16[2240,256]{1,0:T(8,128)(2,1)}) custom-call(s32[6]{0:T(128)} %stack.24.at, bf16[2240,1024]{1,0:T(8,128)(2,1)} %get-tuple-element.93.own, bf16[2240,1024]{1,0:T(8,128)(2,1)} %get-tuple-element.108.near, bf16[256,1536]{1,0:T(8,128)(2,1)} %get-tuple-element.91.refs_0_, ...), custom_call_target="tpu_custom_call" | custom-call | flops 7046430720 | bytes 18907160 | tf_op jit(solution)/shard_map/weight_cols/pallas_call | solution.py:63
  321.8 11.7 %collective-permute-done.43 = bf16[2240,256]{1,0:T(8,128)(2,1)S(1)} collective-permute-done((bf16[2240,256]{1,0:T(8,128)(2,1)S(1)}, bf16[2240,256]{1,0:T(8,128)(2,1)S(1)}, u32[]{:S(2)}, u32[]{:S(2)}) %collective-permute-start.43) | collective-permute-done | bytes 1146912 | tf_op jit(solution)/shard_map/ppermute | solution.py:470
  334.1 11.9 %fusion.16 = f32[1024,1536]{1,0:T(8,128)S(1)} fusion(bf16[2240,1024]{1,0:T(8,128)(2,1)} %get-tuple-element.94.own, bf16[1536,2240]{0,1:T(8,128)(2,1)} %param.27), kind=kOutput, calls=%fused_computation.128 | convolution fusion | flops 7046430720 | bytes 17760256 | tf_op jit(solution)/shard_map/dot_general | solution.py:23
  359.6 13.0 %collective-permute-done.44 = bf16[2240,256]{1,0:T(8,128)(2,1)S(1)} collective-permute-done((bf16[2240,256]{1,0:T(8,128)(2,1)S(1)}, bf16[2240,256]{1,0:T(8,128)(2,1)S(1)}, u32[]{:S(2)}, u32[]{:S(2)}) %collective-permute-start.44) | collective-permute-done | bytes 1146912 | tf_op jit(solution)/shard_map/ppermute | solution.py:470
  399.2 16.2 %collective-permute-done.48 = bf16[2240,256]{1,0:T(8,128)(2,1)S(1)} collective-permute-done((bf16[2240,256]{1,0:T(8,128)(2,1)S(1)}, bf16[2240,256]{1,0:T(8,128)(2,1)S(1)}, u32[]{:S(2)}, u32[]{:S(2)}) %collective-permute-start.48) | collective-permute-done | bytes 1146912 | tf_op jit(solution)/shard_map/ppermute | solution.py:470
  418.0 12.5 %weight_cols.3 = (bf16[2240,256]{1,0:T(8,128)(2,1)}, bf16[2240,256]{1,0:T(8,128)(2,1)}, bf16[2240,256]{1,0:T(8,128)(2,1)}) custom-call(s32[6]{0:T(128)} %stack.24.at, bf16[2240,1024]{1,0:T(8,128)(2,1)} %get-tuple-element.94.own, bf16[2240,1024]{1,0:T(8,128)(2,1)} %get-tuple-element.105.near, bf16[256,1536]{1,0:T(8,128)(2,1)} %get-tuple-element.91.refs_0_, ...), custom_call_target="tpu_custom_call" | custom-call | flops 7046430720 | bytes 18907160 | tf_op jit(solution)/shard_map/weight_cols/pallas_call | solution.py:63
  446.7 12.5 %collective-permute-done.50 = bf16[2240,256]{1,0:T(8,128)(2,1)S(1)} collective-permute-done((bf16[2240,256]{1,0:T(8,128)(2,1)S(1)}, bf16[2240,256]{1,0:T(8,128)(2,1)S(1)}, u32[]{:S(2)}, u32[]{:S(2)}) %collective-permute-start.50) | collective-permute-done | bytes 1146912 | tf_op jit(solution)/shard_map/ppermute | solution.py:470
  472.3 17.6 %collective-permute-done.63.refs_5_ = bf16[256,1536]{1,0:T(8,128)(2,1)} collective-permute-done((bf16[256,1536]{1,0:T(8,128)(2,1)}, bf16[256,1536]{1,0:T(8,128)(2,1)}, u32[]{:S(2)}, u32[]{:S(2)}) %collective-permute-start.63) | collective-permute-done | bytes 786464 | tf_op jit(solution)/shard_map/ppermute | solution.py:423
  498.5 21.0 %collective-permute-done.54 = bf16[2240,256]{1,0:T(8,128)(2,1)S(1)} collective-permute-done((bf16[2240,256]{1,0:T(8,128)(2,1)S(1)}, bf16[2240,256]{1,0:T(8,128)(2,1)S(1)}, u32[]{:S(2)}, u32[]{:S(2)}) %collective-permute-start.54) | collective-permute-done | bytes 1146912 | tf_op jit(solution)/shard_map/ppermute | solution.py:470
  522.1 14.8 %attend_backward.1 = (bf16[256,1536]{1,0:T(8,128)(2,1)}, bf16[8,2,2,128,256]{4,3,2,1,0:T(8,128)(2,1)}) custom-call(bf16[256,1536]{1,0:T(8,128)(2,1)} %query.1.q_ref, bf16[8,2,2,128,256]{4,3,2,1,0:T(8,128)(2,1)} %bitcast.69, bf16[256,1536]{1,0:T(8,128)(2,1)} %get-tuple-element.95.go_ref, s32[128,1]{1,0:T(8,128)} %copy.38.qpos, s32[1,1024]{1,0:T(1,128)} %fusion.4.kpos, ...), custom_call_target="tpu_custom_call" | custom-call | flops 4026531840 | bytes 6689280 | tf_op jit(solution)/shard_map/attend_backward/pallas_call | solution.py:63
  573.1 41.3 %collective-permute-done.56 = bf16[2240,256]{1,0:T(8,128)(2,1)} collective-permute-done((bf16[2240,256]{1,0:T(8,128)(2,1)S(1)}, bf16[2240,256]{1,0:T(8,128)(2,1)}, u32[]{:S(2)}, u32[]{:S(2)}) %collective-permute-start.56) | collective-permute-done | bytes 1146912 | tf_op jit(solution)/shard_map/ppermute | solution.py:470
  617.7 14.7 %collective-permute-done.31.refs_5_ = bf16[256,1536]{1,0:T(8,128)(2,1)S(1)} collective-permute-done((bf16[256,1536]{1,0:T(8,128)(2,1)S(1)}, bf16[256,1536]{1,0:T(8,128)(2,1)S(1)}, u32[]{:S(2)}, u32[]{:S(2)}) %collective-permute-start.31) | collective-permute-done | bytes 786464 | tf_op jit(solution)/shard_map/ppermute | solution.py:423
  671.7 22.4 %collective-permute-done.67 = bf16[2240,256]{1,0:T(8,128)(2,1)S(1)} collective-permute-done((bf16[2240,256]{1,0:T(8,128)(2,1)}, bf16[2240,256]{1,0:T(8,128)(2,1)S(1)}, u32[]{:S(2)}, u32[]{:S(2)}) %collective-permute-start.67) | collective-permute-done | bytes 1146912 | tf_op jit(solution)/shard_map/ppermute | solution.py:470
  778.1 15.8 %collective-permute-done.80.refs_4_ = bf16[2240,256]{1,0:T(8,128)(2,1)S(1)} collective-permute-done((bf16[2240,256]{1,0:T(8,128)(2,1)S(1)}, bf16[2240,256]{1,0:T(8,128)(2,1)S(1)}, u32[]{:S(2)}, u32[]{:S(2)}) %collective-permute-start.80) | collective-permute-done | bytes 1146912 | tf_op jit(solution)/shard_map/ppermute | solution.py:423
  816.3 12.9 %collective-permute-done.84.refs_5_ = bf16[2240,256]{1,0:T(8,128)(2,1)} collective-permute-done((bf16[2240,256]{1,0:T(8,128)(2,1)}, bf16[2240,256]{1,0:T(8,128)(2,1)}, u32[]{:S(2)}, u32[]{:S(2)}) %collective-permute-start.84) | collective-permute-done | bytes 1146912 | tf_op jit(solution)/shard_map/ppermute | solution.py:423
  (419 shorter events, 416.1 us)
Async XLA Ops:
  7.2 105.7 %all-gather.5.cloned.1.call-start = ((), (), s32[]{:S(2)}) async-start(), calls=%async_computation.1 | async-start | bytes 2359296 | tf_op jit(solution)/shard_map/all_gather | solution.py:570
  32.2 68.7 %collective-permute-start.6 = (bf16[384,1536]{1,0:T(8,128)(2,1)S(1)}, bf16[384,1536]{1,0:T(8,128)(2,1)}, u32[]{:S(2)}, u32[]{:S(2)}) collective-permute-start(bf16[384,1536]{1,0:T(8,128)(2,1)S(1)} %copy-done.1), channel_id=1, source_target_pairs={{0,2},{1,3},{2,0},{3,1},{4,6},{5,7},{6,4},{7,5},{8,10},{9,11},{10,... | collective-permute-start | bytes 3538952 | tf_op jit(solution)/shard_map/ppermute | solution.py:423
  32.7 68.2 %collective-permute-start.9 = (bf16[256,1536]{1,0:T(8,128)(2,1)}, bf16[256,1536]{1,0:T(8,128)(2,1)S(1)}, u32[]{:S(2)}, u32[]{:S(2)}) collective-permute-start(bf16[256,1536]{1,0:T(8,128)(2,1)} %bitcast.47), channel_id=1, source_target_pairs={{0,2},{1,3},{2,0},{3,1},{4,6},{5,7},{6,4},{7,5},{8,10},{9,11},{10,... | collective-permute-start | bytes 2359304 | tf_op jit(solution)/shard_map/ppermute | solution.py:423
  34.2 67.3 %collective-permute-start.4 = (bf16[384,1536]{1,0:T(8,128)(2,1)S(1)}, bf16[384,1536]{1,0:T(8,128)(2,1)S(1)}, u32[]{:S(2)}, u32[]{:S(2)}) collective-permute-start(bf16[384,1536]{1,0:T(8,128)(2,1)S(1)} %copy-done.2), channel_id=1, source_target_pairs={{0,1},{1,0},{2,3},{3,2},{4,5},{5,4},{6,7},{7,6},{8,9},{9,8},{10,11... | collective-permute-start | bytes 3538952 | tf_op jit(solution)/shard_map/ppermute | solution.py:423
  34.2 67.2 %collective-permute-start.12 = (bf16[256,1536]{1,0:T(8,128)(2,1)}, bf16[256,1536]{1,0:T(8,128)(2,1)}, u32[]{:S(2)}, u32[]{:S(2)}) collective-permute-start(bf16[256,1536]{1,0:T(8,128)(2,1)} %bitcast.48), channel_id=1, source_target_pairs={{0,4},{4,0},{8,12},{12,8},{16,20},{20,16},{24,28},{28,24},{1,5},{5... | collective-permute-start | bytes 2359304 | tf_op jit(solution)/shard_map/ppermute | solution.py:423
  59.6 47.7 %collective-permute-start.5 = (bf16[384,1536]{1,0:T(8,128)(2,1)}, bf16[384,1536]{1,0:T(8,128)(2,1)}, u32[]{:S(2)}, u32[]{:S(2)}) collective-permute-start(bf16[384,1536]{1,0:T(8,128)(2,1)} %collective-permute-done.3.refs_1_), channel_id=1, source_target_pairs={{0,1},{1,0},{2,3},{3,2},{4,5},{5,4},{6,7},{7,6},{8,9},{9,8},{10,11... | collective-permute-start | bytes 3538952 | tf_op jit(solution)/shard_map/ppermute | solution.py:423
  133.0 39.5 %collective-permute-start.17 = (bf16[256,1536]{1,0:T(8,128)(2,1)}, bf16[256,1536]{1,0:T(8,128)(2,1)S(1)}, u32[]{:S(2)}, u32[]{:S(2)}) collective-permute-start(bf16[256,1536]{1,0:T(8,128)(2,1)} %get-tuple-element.91.refs_0_), channel_id=1, source_target_pairs={{0,1},{1,0},{2,3},{3,2},{4,5},{5,4},{6,7},{7,6},{8,9},{9,8},{10,11... | collective-permute-start | bytes 2359304 | tf_op jit(solution)/shard_map/ppermute | solution.py:423
  385.8 47.3 %collective-permute-start.21 = (bf16[512,1536]{1,0:T(8,128)(2,1)}, bf16[512,1536]{1,0:T(8,128)(2,1)}, u32[]{:S(2)}, u32[]{:S(2)}) collective-permute-start(bf16[512,1536]{1,0:T(8,128)(2,1)} %slice.104), channel_id=1, source_target_pairs={{0,1},{1,0},{2,3},{3,2},{4,5},{5,4},{6,7},{7,6},{8,9},{9,8},{10,11... | collective-permute-start | bytes 4718600 | tf_op jit(solution)/shard_map/ppermute | solution.py:423
  472.3 90.8 %collective-permute-start.64 = (bf16[256,1536]{1,0:T(8,128)(2,1)}, bf16[256,1536]{1,0:T(8,128)(2,1)}, u32[]{:S(2)}, u32[]{:S(2)}) collective-permute-start(bf16[256,1536]{1,0:T(8,128)(2,1)} %get-tuple-element.137.refs_4_), channel_id=1, source_target_pairs={{0,1},{1,0},{2,3},{3,2},{4,5},{5,4},{6,7},{7,6},{8,9},{9,8},{10,11... | collective-permute-start | bytes 2359304 | tf_op jit(solution)/shard_map/ppermute | solution.py:423
  489.9 73.2 %collective-permute-start.65 = (bf16[256,1536]{1,0:T(8,128)(2,1)}, bf16[256,1536]{1,0:T(8,128)(2,1)}, u32[]{:S(2)}, u32[]{:S(2)}) collective-permute-start(bf16[256,1536]{1,0:T(8,128)(2,1)} %collective-permute-done.63.refs_5_), channel_id=1, source_target_pairs={{0,1},{1,0},{2,3},{3,2},{4,5},{5,4},{6,7},{7,6},{8,9},{9,8},{10,11... | collective-permute-start | bytes 2359304 | tf_op jit(solution)/shard_map/ppermute | solution.py:423
  522.1 46.8 %collective-permute-start.57 = (bf16[2240,256]{1,0:T(8,128)(2,1)}, bf16[2240,256]{1,0:T(8,128)(2,1)}, u32[]{:S(2)}, u32[]{:S(2)}) collective-permute-start(bf16[2240,256]{1,0:T(8,128)(2,1)} %broadcast_select_fusion.6), channel_id=1, source_target_pairs={{0,8},{4,12},{24,16},{28,20},{8,0},{12,4},{16,24},{20,28},{1,9},{5... | collective-permute-start | bytes 3440648 | tf_op jit(solution)/shard_map/ppermute | solution.py:470
  536.8 114.1 %all-to-all-start = ((bf16[8,2,2,128,256]{4,3,2,1,0:T(8,128)(2,1)}), bf16[8,2,2,128,256]{4,3,2,1,0:T(8,128)(2,1)}, u32[]{:S(2)}, u32[]{:S(2)}) async-start(bf16[8,2,2,128,256]{4,3,2,1,0:T(8,128)(2,1)} %get-tuple-element.97), calls=%async_computation | async-start | bytes 4194304 | tf_op jit(solution)/shard_map/all_to_all | solution.py:624
  551.1 63.3 %collective-permute-start.56 = (bf16[2240,256]{1,0:T(8,128)(2,1)S(1)}, bf16[2240,256]{1,0:T(8,128)(2,1)}, u32[]{:S(2)}, u32[]{:S(2)}) collective-permute-start(bf16[2240,256]{1,0:T(8,128)(2,1)S(1)} %add_convert_fusion.7), channel_id=1, source_target_pairs={{8,16},{12,20},{16,8},{20,12},{9,17},{13,21},{17,9},{21,13},{10,18... | collective-permute-start | bytes 3440648 | tf_op jit(solution)/shard_map/ppermute | solution.py:470
  561.8 55.9 %collective-permute-start.28 = (bf16[256,384]{1,0:T(8,128)(2,1)}, bf16[256,384]{1,0:T(8,128)(2,1)}, u32[]{:S(2)}, u32[]{:S(2)}) collective-permute-start(bf16[256,384]{1,0:T(8,128)(2,1)} %get-tuple-element.177), channel_id=1, source_target_pairs={{0,2},{1,3},{2,0},{3,1},{4,6},{5,7},{6,4},{7,5},{8,10},{9,11},{10,... | collective-permute-start | bytes 589832 | tf_op jit(solution)/shard_map/ppermute | solution.py:423
  563.1 73.6 %collective-permute-start.29 = (bf16[256,384]{1,0:T(8,128)(2,1)}, bf16[256,384]{1,0:T(8,128)(2,1)}, u32[]{:S(2)}, u32[]{:S(2)}) collective-permute-start(bf16[256,384]{1,0:T(8,128)(2,1)} %get-tuple-element.176), channel_id=1, source_target_pairs={{0,1},{1,0},{2,3},{3,2},{4,5},{5,4},{6,7},{7,6},{8,9},{9,8},{10,11... | collective-permute-start | bytes 589832 | tf_op jit(solution)/shard_map/ppermute | solution.py:423
  563.1 73.6 %collective-permute-start.30 = (bf16[256,384]{1,0:T(8,128)(2,1)}, bf16[256,384]{1,0:T(8,128)(2,1)}, u32[]{:S(2)}, u32[]{:S(2)}) collective-permute-start(bf16[256,384]{1,0:T(8,128)(2,1)} %get-tuple-element.175), channel_id=1, source_target_pairs={{0,3},{1,2},{2,1},{3,0},{4,7},{5,6},{6,5},{7,4},{8,11},{9,10},{10,... | collective-permute-start | bytes 589832 | tf_op jit(solution)/shard_map/ppermute | solution.py:423
  568.9 63.5 %collective-permute-start.58 = (bf16[2240,256]{1,0:T(8,128)(2,1)S(1)}, bf16[2240,256]{1,0:T(8,128)(2,1)S(1)}, u32[]{:S(2)}, u32[]{:S(2)}) collective-permute-start(bf16[2240,256]{1,0:T(8,128)(2,1)S(1)} %copy-done.8), channel_id=1, source_target_pairs={{0,4},{4,0},{8,12},{12,8},{16,20},{20,16},{24,28},{28,24},{1,5},{5... | collective-permute-start | bytes 3440648 | tf_op jit(solution)/shard_map/ppermute | solution.py:423
  643.4 58.3 %collective-permute-start.34 = (bf16[384,768]{1,0:T(8,128)(2,1)}, bf16[384,768]{1,0:T(8,128)(2,1)}, u32[]{:S(2)}, u32[]{:S(2)}) collective-permute-start(bf16[384,768]{1,0:T(8,128)(2,1)} %get-tuple-element.104), channel_id=1, source_target_pairs={{0,4},{4,0},{8,12},{12,8},{16,20},{20,16},{24,28},{28,24},{1,5},{5... | collective-permute-start | bytes 1769480 | tf_op jit(solution)/shard_map/ppermute | solution.py:423
  653.6 49.6 %collective-permute-start.74 = (bf16[256,512]{1,0:T(8,128)(2,1)}, bf16[256,512]{1,0:T(8,128)(2,1)}, u32[]{:S(2)}, u32[]{:S(2)}) collective-permute-start(bf16[256,512]{1,0:T(8,128)(2,1)} %grad_kv.1.gkv.refs_4_), channel_id=1, source_target_pairs={{0,2},{1,3},{2,0},{3,1},{4,6},{5,7},{6,4},{7,5},{8,10},{9,11},{10,... | collective-permute-start | bytes 786440 | tf_op jit(solution)/shard_map/ppermute | solution.py:423
  710.0 55.9 %collective-permute-start.25 = (f32[1,1280]{1,0:T(1,128)S(1)}, f32[1,1280]{1,0:T(1,128)S(1)}, u32[]{:S(2)}, u32[]{:S(2)}) collective-permute-start(f32[1,1280]{1,0:T(1,128)S(1)} %fusion.3), channel_id=1, source_target_pairs={{0,4},{4,0},{8,12},{12,8},{16,20},{20,16},{24,28},{28,24},{1,5},{5... | collective-permute-start | bytes 15368 | tf_op jit(solution)/shard_map/ppermute | solution.py:423
  714.5 51.5 %collective-permute-start.77 = (bf16[384,256]{1,0:T(8,128)(2,1)}, bf16[384,256]{1,0:T(8,128)(2,1)S(1)}, u32[]{:S(2)}, u32[]{:S(2)}) collective-permute-start(bf16[384,256]{1,0:T(8,128)(2,1)} %get-tuple-element.148), channel_id=1, source_target_pairs={{0,4},{4,0},{8,12},{12,8},{16,20},{20,16},{24,28},{28,24},{1,5},{5... | collective-permute-start | bytes 589832 | tf_op jit(solution)/shard_map/ppermute | solution.py:423
  765.9 37.8 %collective-permute-start.19 = (bf16[512,1536]{1,0:T(8,128)(2,1)S(1)}, bf16[512,1536]{1,0:T(8,128)(2,1)S(1)}, u32[]{:S(2)}, u32[]{:S(2)}) collective-permute-start(bf16[512,1536]{1,0:T(8,128)(2,1)S(1)} %slice.100), channel_id=1, source_target_pairs={{0,1},{1,0},{2,3},{3,2},{4,5},{5,4},{6,7},{7,6},{8,9},{9,8},{10,11... | collective-permute-start | bytes 4718600 | tf_op jit(solution)/shard_map/ppermute | solution.py:423
  766.0 40.0 %collective-permute-start.26 = (f32[1,1280]{1,0:T(1,128)S(1)}, f32[1,1280]{1,0:T(1,128)S(1)}, u32[]{:S(2)}, u32[]{:S(2)}) collective-permute-start(f32[1,1280]{1,0:T(1,128)S(1)} %add.223), channel_id=1, source_target_pairs={{0,8},{4,12},{8,0},{12,4},{16,24},{20,28},{24,16},{28,20},{1,9},{5... | collective-permute-start | bytes 15368 | tf_op jit(solution)/shard_map/ppermute | solution.py:423
  829.3 35.5 %collective-permute-start.85 = (bf16[384,768]{1,0:T(8,128)(2,1)}, bf16[384,768]{1,0:T(8,128)(2,1)}, u32[]{:S(2)}, u32[]{:S(2)}) collective-permute-start(bf16[384,768]{1,0:T(8,128)(2,1)} %add_convert_fusion.19), channel_id=1, source_target_pairs={{8,0},{12,4},{16,24},{20,28},{9,1},{13,5},{17,25},{21,29},{10,2},{... | collective-permute-start | bytes 1769480 | tf_op jit(solution)/shard_map/ppermute | solution.py:470
  (136 other events, 2449.9 us)
Sparse Core Ops, SparseCore 0:
  30.7 52.9 all-gather.4

commit v2 on v1

--- a/solution.py
+++ b/solution.py
@@ -287,40 +287,89 @@
     )
 
 
-def weight_cols_kernel(n, tiles, at, own, near, *refs):
-    xs, outs, x = refs[:n], refs[n : n + tiles], refs[n + tiles]
-    rows = xs[0].shape[0]
-    half = x.shape[1]
+def weight_tiles_kernel(n, m, flip, at, *refs):
+    hs, xs, outs, x = refs[:m], refs[m : m + n], refs[m + n : -1], refs[-1]
+    rows, width = xs[0].shape
+    size = x.shape[1]
 
     @pl.when(pl.program_id(0) == 0)
     def _():
+        first = (at[0] ^ flip) * size
         for p in range(n):
-            x[p * rows : (p + 1) * rows, :] = lanes(xs[p], at[0], half)[...]
-
-    mid = own.shape[1]
-    total = dot_nn(own[...], x[:mid, :]) + dot_nn(near[...], x[mid:, :])
-    tile = half // tiles
-    for i in range(tiles):
-        outs[i][...] = total[:, i * tile : (i + 1) * tile].astype(BF)
-
-
-def weight_cols(at, xs, own, near, tiles):
+            x[p * rows : (p + 1) * rows, :] = xs[p][:, pl.ds(pl.multiple_of(first, 128), size)]
+
+    total, row = 0.0, 0
+    for h in hs:
+        total = total + dot_nn(h[...], x[row : row + h.shape[1], :])
+        row += h.shape[1]
+    total = total.astype(BF)
+    for i, out in enumerate(outs):
+
+        @pl.when(pl.program_id(0) == i)
+        def _():
+            out[...] = total
+
+
+TILES = 4
+
+
+def weight_tiles(at, xs, hs, flip=0):
     n = len(xs)
     rows, width = xs[0].shape
-    half = width // 2
-    wide, cols = own.shape
+    wide = hs[0].shape[0]
+    tile = wide // TILES
+    return call(
+        functools.partial(weight_tiles_kernel, n, len(hs), flip),
+        "weight_tiles",
+        (at, *hs, *xs),
+        [SCALARS]
+        + [pl.BlockSpec((tile, h.shape[1]), lambda i: (i, 0)) for h in hs]
+        + [fixed(a) for a in xs],
+        [shape((tile, width // 2), BF)] * TILES,
+        None,
+        (TILES,),
+        n * rows * width * wide,
+        scratch=[pltpu.VMEM((n * rows, width // 2), BF)],
+    )
+
+
+def rows_back_kernel(n, *refs):
+    hs, ws, (keep, send, acc) = refs[:n], refs[n : 2 * n], refs[2 * n :]
+    total = dot_tn(hs[0][...], ws[0][...])
+    for h, w in zip(hs[1:], ws[1:]):
+        total = total + dot_tn(h[...], w[...])
+    first = pl.program_id(0) == 0
+
+    @pl.when(first)
+    def _():
+        acc[...] = total
+
+    @pl.when(jnp.logical_not(first))
+    def _():
+        acc[...] = acc[...] + total
+
+    @pl.when(pl.program_id(0) == pl.num_programs(0) - 1)
+    def _():
+        half = keep.shape[0]
+        keep[...] = acc[:half, :]
+        send[...] = acc[half:, :].astype(BF)
+
+
+def rows_back(hs, ws):
+    wide, rows = hs[0].shape
+    width = ws[0].shape[1]
     tile = unit_tile(wide)
-    part = pl.BlockSpec((tile, cols), lambda i: (i, 0))
     return call(
-        functools.partial(weight_cols_kernel, n, tiles),
-        "weight_cols",
-        (at, own, near, *xs),
-        [SCALARS, part, part] + [fixed(a) for a in xs],
-        [shape((wide, half // tiles), BF)] * tiles,
-        [pl.BlockSpec((tile, half // tiles), lambda i: (i, 0))] * tiles,
+        functools.partial(rows_back_kernel, len(hs)),
+        "rows_back",
+        (*hs, *ws),
+        [pl.BlockSpec((tile, rows), lambda i: (i, 0))] * len(hs)
+        + [pl.BlockSpec((tile, width), lambda i: (i, 0))] * len(ws),
+        [shape((rows // 2, width), F32), shape((rows // 2, width), BF)],
+        None,
         (wide // tile,),
-        2 * n * rows * half * wide,
-        scratch=[pltpu.VMEM((n * rows, half), BF)],
+        2 * len(hs) * wide * rows * width,
+        scratch=[pltpu.VMEM((rows, width), F32)],
     )
 
 
@@ -340,12 +389,10 @@
 
 
 def grad_kv_kernel(recv, table, out):
-    n_ctx, seq, _, toks, _ = recv.shape
+    seq, _, toks, _ = recv.shape
     for k in range(KV_HEADS):
         for s in range(seq):
-            total = recv[0, s, k].astype(F32)
-            for c in range(1, n_ctx):
-                total = total + recv[c, s, k].astype(F32)
+            total = recv[s, k].astype(F32)
             at = slice(s * toks, (s + 1) * toks)
             out[at, k * HEAD : (k + 1) * HEAD] = turn(total[:, :HEAD], table[...], -1.0).astype(BF)
             out[at, (KV_HEADS + k) * HEAD : (KV_HEADS + k + 1) * HEAD] = total[:, HEAD:].astype(BF)
@@ -368,53 +415,88 @@
     gi_ref[...] = gm[...] + scale * a - v * (scale**3 * jnp.mean(a * v, -1, keepdims=True))
 
 
-def split_weight_kernel(n, at, *refs):
-    xs, gs, (keep, send) = refs[:n], refs[n : 2 * n], refs[2 * n :]
-    half = keep.shape[1]
-    for out, which in ((keep, at[0]), (send, 1 - at[0])):
-        total = dot_tn(xs[0][...], lanes(gs[0], which, half)[...])
-        for p in range(1, n):
-            total = total + dot_tn(xs[p][...], lanes(gs[p], which, half)[...])
-        out[...] = total.astype(out.dtype)
-
-
-def split_weight(at, xs, gs):
-    part, wide = xs[0].shape[1], gs[0].shape[1]
-    args = (at, *xs, *gs)
+def attention_weights_kernel(n_out, n_query, at, attn, normed, *refs):
+    branches, queries, kvs = refs[:n_out], refs[n_out : n_out + n_query], refs[n_out + n_query : -4]
+
+    def product(x, pieces, which, size):
+        total, row = 0.0, 0
+        for g in pieces:
+            total = total + dot_tn(x[row : row + g.shape[0], :], lanes(g, which, size)[...])
+            row += g.shape[0]
+        return total.astype(BF)
+
+    part, half = attn.shape[1], branches[0].shape[1] // 2
+    for outs, which in ((refs[-4:-2], at[0]), (refs[-2:], 1 - at[0])):
+        outs[0][:part, :] = product(attn, branches, which, half)
+        kv = product(normed, kvs, which, kvs[0].shape[1] // 2)
+        cuts = half // kv.shape[1]
+        rows = part // cuts
+        for j in range(cuts):
+            outs[0][part : part + rows, j * kv.shape[1] : (j + 1) * kv.shape[1]] = kv[
+                j * rows : (j + 1) * rows
+            ]
+        outs[0][part + rows :, :] = jnp.zeros((outs[0].shape[0] - part - rows, half), BF)
+        outs[1][...] = product(normed, queries, which, half)
+
+
+def attention_weights(at, rows, attn, normed, branches, queries, kvs):
+    part, half = attn.shape[1], branches[0].shape[1] // 2
+    args = (at, attn, normed, *branches, *queries, *kvs)
     return call(
-        functools.partial(split_weight_kernel, len(xs)),
-        "split_weight",
+        functools.partial(attention_weights_kernel, len(branches), len(queries)),
+        "attention_weights",
         args,
         [SCALARS] + [whole(a) for a in args[1:]],
-        [shape((part, wide // 2), F32), shape((part, wide // 2), BF)],
-        flops=2 * len(xs) * xs[0].shape[0] * part * wide,
-    )
-
-
-def join_kernel(tiles, at, *refs):
-    mine, theirs, out = refs[:tiles], refs[tiles : 2 * tiles], refs[2 * tiles]
-    tile = mine[0].shape[1]
-    for j in range(2 * tiles):
-        for side, ref in ((0, mine), (1, theirs)):
-
-            @pl.when((at[0] ^ side) == j // tiles)
-            def _():
-                out[:, j * tile : (j + 1) * tile] = ref[j % tiles][...].astype(F32)
+        [shape((rows, half), BF), shape((part, half), BF)] * 2,
+        flops=2 * attn.shape[0] * part * 7 * half,
+    )
+
+
+def relay_kernel(flag, fresh, went, arrived, summed, across, sent, go_on, out, done):
+    @pl.when(flag[0] == 1)
+    def _():
+        out[...] = fresh[...]
+        done[...] = arrived[...]
+
+    @pl.when(flag[0] == 0)
+    def _():
+        go_on[...] = (went[...].astype(F32) + arrived[...].astype(F32)).astype(BF)
+        out[...] = (summed[...].astype(F32) + across[...].astype(F32)).astype(BF)
+        done[...] = sent[...]
+
+
+def relay(flag, arrays):
+    return call(
+        relay_kernel,
+        "relay",
+        (flag, *arrays),
+        [SCALARS] + [whole(a) for a in arrays],
+        [shape(arrays[0].shape, BF)] * 3,
+    )
+
+
+def join_kernel(at, *refs):
+    mine, theirs, out = refs[:TILES], refs[TILES:-1], refs[-1]
+    cut = mine[0].shape[1]
+    for i in range(TILES):
+        for side, tiles in ((0, mine), (1, theirs)):
+            for half in range(2):
+
+                @pl.when((pl.program_id(0) == i) & ((at[0] ^ side) == half))
+                def _():
+                    out[:, half * cut : (half + 1) * cut] = tiles[i][...].astype(F32)
 
 
 def join(at, mine, theirs):
-    tiles = len(mine)
-    wide, cols = mine[0].shape
-    tile = unit_tile(wide)
-    part = pl.BlockSpec((tile, cols), lambda i: (i, 0))
+    rows, cols = mine[0].shape
     return call(
-        functools.partial(join_kernel, tiles),
+        join_kernel,
         "join",
         (at, *mine, *theirs),
-        [SCALARS] + [part] * (2 * tiles),
-        [shape((wide, 2 * tiles * cols), F32)],
-        [pl.BlockSpec((tile, 2 * tiles * cols), lambda i: (i, 0))],
-        (wide // tile,),
+        [SCALARS] + [fixed(a) for a in (*mine, *theirs)],
+        [shape((TILES * rows, 2 * cols), F32)],
+        [pl.BlockSpec((rows, 2 * cols), lambda i: (i, 0))],
+        (TILES,),
     )[0]
 
 
@@ -432,83 +514,149 @@
     return order
 
 
-def gather_dp(value):
-    blocks = [value]
-    step = lax.axis_size("dp") // 2
-    while step:
-        blocks += [swap(b, "dp", step) for b in blocks]
-        step //= 2
-    return blocks
-
-
-def exchange_dp(value, part):
-    here = lax.axis_index("dp")
-    out = [lax.dynamic_slice_in_dim(value, here * part, part, 1)]
-    for offset in offsets_of(lax.axis_size("dp"))[1:]:
-        theirs = lax.dynamic_slice_in_dim(value, (here ^ offset) * part, part, 1)
-        out.append(swap(theirs, "dp", offset))
-    return out
-
-
-def scatter_dp(value):
-    size = lax.axis_size("dp")
-    step = 1
-    while step < size:
-        half = value.shape[0] // 2
-        value = value[:half].astype(F32) + swap(value[half:].astype(BF), "dp", step).astype(F32)
-        step *= 2
-    return value
-
-
-def ctx_sums(blocks):
-    length = lax.axis_size("ctx") // 2
-    last = length - 1
-    place = lax.axis_index("ctx") // 2
-    depth = length // 2 - 1
-
-    def send(value, pairs):
+def tie(values, others):
+    return lax.optimization_barrier((values, others))[0]
+
+
+def swaps(moves, first=(), beside=()):
+    sent = tie([m[0] for m in moves], list(first))
+    got = [swap(v, *where) for v, (_, *where) in zip(sent, moves)]
+    return lax.optimization_barrier((got, list(beside)))[0]
+
+
+class CtxSums:
+    GAP = 2
+
+    def __init__(self, block):
+        self.length = lax.axis_size("ctx") // 2
+        self.depth = self.length // 2 - 1
+        self.place = lax.axis_index("ctx") // 2
+        self.number = 0
+        self.own, self.other = {}, {}
+        self.final = self.own if self.depth != 1 else {}
+        self.got, self.arrived = [], []
+        ends = (self.place == 0) | (self.place == self.length - 1)
+        self.flag = ends.astype(jnp.int32)[None]
+        self.sums, self.sends = {}, {}
+        self.own[0] = block
+        self.moves = self.plan(0)
+
+    def send(self, value, pairs):
         return lax.ppermute(
             value, "ctx", [(2 * i + y, 2 * j + y) for i, j in pairs for y in range(2)]
         )
 
-    n = len(blocks)
-    state = list(blocks)
-    other = [None] * n
-    before = []
-    n_stage = 2 * depth + 2
-    for slot in range(n + n_stage - 1):
+    def plan(self, now):
+        if self.depth == 1:
+            return self.short_plan(now)
+        last, own = self.length - 1, self.own
         moves = []
-        for j in range(depth):
-            going, coming = slot - j, slot - (2 * depth - j)
-            has_in, has_out = 0 <= going < n, 0 <= coming < n
+        for j in range(self.depth):
+            going, coming = now - self.GAP * j, now - self.GAP * (2 * self.depth - j)
             inward = [(j, j + 1), (last - j, last - j - 1)]
             outward = [(b, a) for a, b in inward]
-            outer = (place == j) | (place == last - j)
-            if has_in and has_out and state[going].shape == state[coming].shape:
-                value = jnp.where(outer, state[going], state[coming])
+            outer = (self.place == j) | (self.place == last - j)
+            if going in own and coming in own:
+                value = jnp.where(outer, own[going], own[coming])
                 moves.append((value, inward + outward, going, coming, outer))
+            elif going in own:
+                moves.append((own[going], inward, going, None, outer))
+            elif coming in own:
+                moves.append((own[coming], outward, None, coming, outer))
+        b = now - self.GAP * self.depth
+        if b in own:
+            across = [(self.depth, self.depth + 1), (self.depth + 1, self.depth)]
+            moves.append((own[b], across, b, None, None))
+        b = now - self.GAP * (2 * self.depth + 1)
+        if b in own:
+            moves.append((own[b], None, b, None, None))
+        return moves
+
+    def short_plan(self, now):
+        own, ends, middle = self.own, [(0, 1), (3, 2)], [(1, 2), (2, 1)]
+        entering, leaving = now in own, now - 2 * self.GAP in own
+        moves = []
+        if entering and not leaving:
+            self.sends[now] = own[now]
+        if entering or leaving:
+            pairs = (ends if entering else []) + ([(b, a) for a, b in ends] if leaving else [])
+            moves.append((self.sends[now], pairs, "ends", now, None))
+        if now - self.GAP in own:
+            moves.append((self.sums[now - self.GAP], middle, "middle", now, None))
+        if now - 3 * self.GAP in own:
+            b = now - 3 * self.GAP
+            moves.append((self.final[b], None, b, None, None))
+        return moves
+
+    def short_settle(self):
+        now, ends, middle = None, None, None
+        for got, (_, pairs, kind, at, _) in self.arrived:
+            if pairs is None:
+                self.other[kind] = got
                 continue
-            if has_in:
-                moves.append((state[going], inward, going, None, outer))
-            if has_out:
-                moves.append((state[coming], outward, None, coming, outer))
-        if 0 <= slot - depth < n:
-            b = slot - depth
-            moves.append((state[b], [(depth, depth + 1), (depth + 1, depth)], b, None, None))
-        if 0 <= slot - n_stage + 1 < n:
-            moves.append((state[slot - n_stage + 1], None, None, None, None))
-        sent, _ = lax.optimization_barrier(([m[0] for m in moves], before))
-        before = []
-        for value, (_, pairs, going, coming, outer) in zip(sent, moves):
-            got = swap(value, "ctx", 1) if pairs is None else send(value, pairs)
-            before.append(got)
+            now = at
+            if kind == "ends":
+                ends = got
+            else:
+                middle = got
+        self.arrived = []
+        if now is None:
+            return
+        own = self.own
+        fresh, went = own.get(now + self.GAP), own.get(now)
+        summed, sent = self.sums.get(now - self.GAP), self.sends.get(now)
+        if went is not None and middle is None and fresh is not None:
+            self.sums[now] = (went.astype(F32) + ends.astype(F32)).astype(BF)
+            return
+        fill = next(a for a in (ends, middle) if a is not None)
+        arrays = [fill if a is None else a for a in (fresh, went, ends, summed, middle, sent)]
+        self.sums[now], self.sends[now + self.GAP], self.final[now - 2 * self.GAP] = relay(
+            self.flag, arrays
+        )
+
+    def settle(self):
+        if self.depth == 1:
+            return self.short_settle()
+        own = self.own
+        for got, (_, pairs, going, coming, outer) in self.arrived:
             if pairs is None:
-                other[slot - n_stage + 1] = got
+                self.other[going] = got
+                continue
             if going is not None:
-                state[going] = (state[going].astype(F32) + got.astype(F32)).astype(BF)
+                own[going] = (own[going].astype(F32) + got.astype(F32)).astype(BF)
             if coming is not None:
-                state[coming] = jnp.where(outer, got, state[coming])
-    return state, other
+                own[coming] = jnp.where(outer, got, own[coming])
+        self.arrived = []
+
+    def slot(self, first=(), extra=(), upcoming=None, beside=()):
+        now, moves = self.number, self.moves
+        self.number += 1
+        sent, more = tie(([m[0] for m in moves], [e[0] for e in extra]), (self.got, list(first)))
+        got = [
+            swap(value, "ctx", 1) if pairs is None else self.send(value, pairs)
+            for value, (_, pairs, *_) in zip(sent, moves)
+        ]
+        got += [swap(value, *where) for value, (_, *where) in zip(more, extra)]
+        if upcoming is not None:
+            self.own[now + 1] = upcoming()
+        self.settle()
+        self.moves = self.plan(now + 1)
+        got, ready, _ = lax.optimization_barrier((got, [m[0] for m in self.moves], list(beside)))
+        self.moves = [(v, *m[1:]) for v, m in zip(ready, self.moves)]
+        self.got = got
+        self.arrived = list(zip(got, moves))
+        return got[len(moves) :]
+
+    def exchanged(self, block):
+        if block in self.other:
+            return self.other[block]
+        for got, (_, pairs, number, *_) in self.arrived:
+            if pairs is None and number == block:
+                return got
+        return None
+
+    def after(self, values):
+        return tie(values, self.got)
 
 
 def shards(
@@ -543,19 +691,31 @@
     kpos = key_pos[None, :]
     at = jnp.stack([parity, dp_index] + [dp_index ^ o for o in offsets_of(n_dp)]).astype(jnp.int32)
 
-    small = lax.all_gather(
-        jnp.concatenate([gain_attn, gain_mlp, b_query, b_key, b_value])[None], "dp", axis=0, tiled=True
-    )
+    far, close = n_dp // 2, 1
     cuts = [0]
     for item in (gain_attn, gain_mlp, b_query, b_key, b_value):
         cuts.append(cuts[-1] + item.shape[0])
+    small = jnp.concatenate([gain_attn, gain_mlp, b_query, b_key, b_value])[None]
+    w_kv = jnp.concatenate([w_key, w_value], 1)
+    small_x, kv_x, small_c, kv_c = swaps(
+        [(small, "dp", far), (w_kv, "dp", far), (small, "dp", close), (w_kv, "dp", close)]
+    )
+    small_xc, kv_xc = swaps([(small_x, "dp", close), (kv_x, "dp", close)])
+    full_kv = [w_kv, kv_x, kv_c, kv_xc]
+    gathered = jnp.concatenate([small, small_x, small_c, small_xc], 0).astype(F32)
+    picks = at[2:][None, :] == jnp.arange(n_dp, dtype=jnp.int32)[:, None]
+    gathered = jnp.sum(jnp.where(picks[:, :, None], gathered[None], 0.0), 1)
     gain_one, gain_two, bias_query, bias_key, bias_value = [
-        small[:, a:b].reshape(1, -1).astype(F32) for a, b in zip(cuts[:-1], cuts[1:])
+        gathered[:, a:b].reshape(1, -1) for a, b in zip(cuts[:-1], cuts[1:])
     ]
     bias_kv = jnp.concatenate([bias_key, bias_value], 1)
-    full_kv = gather_dp(jnp.concatenate([w_key, w_value], 1))
-    full_query = gather_dp(w_query)
-    full_out = gather_dp(w_out)
+
+    turn_of = lax.axis_index("ctx") // 2 % 2
+    grad_rows = cotangent.reshape(rows, width)
+    half_query = lax.dynamic_slice_in_dim(w_query, turn_of * (width // 2), width // 2, 1)
+    half_x, top_y, query_c = swaps(
+        [(half_query, "dp", far), (grad_rows, "ctx", 1), (w_query, "dp", close)], [kv_x]
+    )
 
     inputs = tokens.reshape(rows, width)
     args = (at, inputs, gain_one, bias_kv, table, *full_kv)
@@ -568,6 +728,12 @@
         flops=4 * rows * width * kv_width,
     )
     kv_all = lax.all_gather(kv_own, "ctx", axis=0, tiled=False)
+    half_z, top_x = swaps([(half_x, "ctx", 2), (grad_rows, "dp", far)], [half_x])
+    query_x = jnp.concatenate(
+        [jnp.where(turn_of == 0, half_x, half_z), jnp.where(turn_of == 0, half_z, half_x)], 1
+    )
+    (query_xc,) = swaps([(query_x, "dp", close)])
+    full_query = [w_query, query_x, query_c, query_xc]
     args = (at, normed_one, bias_query, table, *full_query)
     queries = call(
         functools.partial(query_kernel, n_dp),
@@ -577,7 +743,19 @@
         [shape((rows, width), BF)],
         flops=2 * rows * width * width,
     )[0]
+    out_x, out_c, top_xy, top_c = swaps(
+        [(w_out, "dp", far), (w_out, "dp", close), (top_x, "ctx", 1), (grad_rows, "dp", close)],
+        [top_x],
+        [queries],
+    )
     attn_vec = attend_forward(queries, kv_all, qpos, kpos)
+    out_xc, top_xc, top_yc, top_xyc = swaps(
+        [(out_x, "dp", close), (top_x, "dp", close), (top_y, "dp", close), (top_xy, "dp", close)],
+        [out_x],
+        [attn_vec],
+    )
+    full_out = [w_out, out_x, out_c, out_xc]
+    tops = [grad_rows, top_x, top_c, top_xc, top_y, top_xy, top_yc, top_xyc]
     args = (at, inputs, attn_vec, gain_two, *full_out)
     middle, normed_two = call(
         functools.partial(out_norm_kernel, n_dp),
@@ -588,23 +766,52 @@
         flops=2 * rows * width * width,
     )
 
-    grad_rows = cotangent.reshape(rows, width)
-    top_own, top_near = gather_dp(grad_rows), gather_dp(swap(grad_rows, "ctx", 1))
-    norm_own, norm_near = gather_dp(normed_two), gather_dp(swap(normed_two, "ctx", 1))
+    tops = tie(tops, normed_two)
+    grad_hidden = hidden_back(w_down, tops)
+    norm_x, norm_y, norm_c = swaps(
+        [(normed_two, "dp", far), (normed_two, "ctx", 1), (normed_two, "dp", close)],
+        [],
+        [grad_hidden],
+    )
+    (norm_xc,) = swaps([(norm_x, "dp", close)])
     wide_gate, wide_up = w_gate.T, w_up.T
-    grad_hidden = hidden_back(w_down, top_own + top_near)
+    norm_own = [normed_two, norm_x, norm_c, norm_xc]
     hidden, grad_gate, grad_up = units(grad_hidden, 0, wide_gate, wide_up, norm_own)
-    near = units(grad_hidden, 1, wide_gate, wide_up, norm_near)
-    tiles = 3
-    part_down = weight_cols(at, top_own + top_near, hidden, near[0], tiles)
-    part_gate = weight_cols(at, norm_own + norm_near, grad_gate, near[1], tiles)
-    part_up = weight_cols(at, norm_own + norm_near, grad_up, near[2], tiles)
-
-    grad_norm_two = scatter_dp(
-        (matmul(grad_gate, wide_gate, 0, 0) + matmul(grad_up, wide_up, 0, 0)).astype(BF)
-    )
-    mlp_out = scatter_dp(matmul(hidden, w_down, 0, 0).astype(BF))
-    layer_out = (middle + mlp_out).astype(BF).reshape(tokens.shape)
+    norm_yx, norm_yc = swaps(
+        [(norm_y, "dp", far), (norm_y, "dp", close)], [norm_xc], [hidden]
+    )
+    (norm_yxc,) = swaps([(norm_yx, "dp", close)], [norm_xc], [hidden])
+    norms = norm_own + [norm_y, norm_yx, norm_yc, norm_yxc]
+    peers = offsets_of(n_dp)[1:]
+
+    def columns(value):
+        return [
+            (lax.dynamic_slice_in_dim(value, (dp_index ^ o) * part, part, 1), "dp", o) for o in peers
+        ]
+
+    def with_own(value, got):
+        return jnp.concatenate(
+            [lax.dynamic_slice_in_dim(value, dp_index * part, part, 1)] + list(got), 0
+        )
+
+    near = units(grad_hidden, 1, wide_gate, wide_up, norms[n_dp:])
+    down = weight_tiles(at, tops, [hidden, near[0]])
+    line = CtxSums(down[0])
+
+    gate_now, up_now = tie((grad_gate, grad_up), down)
+    partial, sent = rows_back([gate_now, up_now], [wide_gate, wide_up])
+    normed_cols = line.slot(down, columns(normed_one), lambda: down[1], [partial])
+    normed_cols = with_own(normed_one, normed_cols)
+    gn_got, *attn_cols = line.slot(
+        [partial, sent], [(sent, "dp", close)] + columns(attn_vec), lambda: down[2]
+    )
+    attn_cols = with_own(attn_vec, attn_cols)
+    partial = partial + gn_got.astype(F32)
+    sent = partial[rows:].astype(BF)
+    gate_now, near_now = line.after((grad_gate, near[1]))
+    gate = weight_tiles(at, norms, [gate_now, near_now])
+    (gn_got,) = line.slot([sent], [(sent, "dp", far)], lambda: down[3])
+    grad_norm_two = partial[:rows] + gn_got.astype(F32)
 
     args = (at, grad_norm_two, middle, grad_rows, gain_two, *full_out)
     grad_middle, grad_branch, grad_attn, grad_gain_m = call(
@@ -621,7 +828,22 @@
         flops=2 * rows * width * width,
     )
     grad_query, grad_kv_all = attend_backward(queries, kv_all, grad_attn, qpos, kpos, table)
-    recv = lax.all_to_all(grad_kv_all, "ctx", 0, 0, tiled=True)
+    recv = lax.psum_scatter(grad_kv_all, "ctx", scatter_dimension=0, tiled=False)
+    line.slot(gate, [], lambda: gate[0])
+    (branch_x,) = line.slot([grad_query], [(grad_branch, "dp", far)], lambda: gate[1])
+    branches = [jnp.concatenate([grad_branch, branch_x], 0)]
+    up_now, near_now = line.after((grad_up, near[2]))
+    up = weight_tiles(at, norms, [up_now, near_now])
+    query_x, got = line.slot(
+        branches, [(grad_query, "dp", far), (branches[0], "dp", close)], lambda: gate[2]
+    )
+    branches.append(got)
+    queries_back = [jnp.concatenate([grad_query, query_x], 0)]
+    mlp_partial, mlp_sent = rows_back([tie(hidden, (up, line.got))], [w_down])
+    (got,) = line.slot(
+        [*up, *queries_back], [(queries_back[0], "dp", close)], lambda: gate[3]
+    )
+    queries_back.append(got)
     grad_kv = call(
         grad_kv_kernel,
         "grad_kv",
@@ -629,6 +851,11 @@
         [whole(recv), whole(table)],
         [shape((rows, 2 * kv_width), BF)],
     )[0]
+    (mlp_got,) = line.slot([mlp_partial, mlp_sent], [(mlp_sent, "dp", close)], lambda: up[0])
+    mlp_partial = mlp_partial + mlp_got.astype(F32)
+    mlp_sent = mlp_partial[rows:].astype(BF)
+    kvs = line.slot([grad_kv], [(grad_kv, "dp", o) for o in peers], lambda: up[1])
+    kvs = [grad_kv, *kvs]
     args = (at, grad_query, grad_kv, inputs, gain_one, grad_middle, *full_query, *full_kv)
     grad_input, grad_gain_a, grad_bias = call(
         functools.partial(input_back_kernel, n_dp),
@@ -639,52 +866,89 @@
         flops=2 * rows * width * (width + 2 * kv_width),
         scratch=[pltpu.VMEM((rows, width), F32)],
     )
-
-    normed_cols = exchange_dp(normed_one, part)
-    attn_cols = exchange_dp(attn_vec, part)
-    halves = [
-        split_weight(at, attn_cols, gather_dp(grad_branch)),
-        split_weight(at, normed_cols, gather_dp(grad_query)),
-        split_weight(at, normed_cols, gather_dp(grad_kv)),
+    vectors = jnp.concatenate(
+        [
+            v.reshape(n_dp, -1)
+            for v in (
+                grad_gain_a,
+                grad_gain_m,
+                grad_bias[:, :width],
+                grad_bias[:, width : width + kv_width],
+                grad_bias[:, width + kv_width :],
+            )
+        ],
+        1,
+    )
+    shares = [lax.dynamic_slice_in_dim(vectors, at[2 + p], 1, 0) for p in range(n_dp)]
+    tile_rows = down[0].shape[0]
+    out_keep, query_keep, out_send, query_send = attention_weights(
+        at, tile_rows, attn_cols, normed_cols, branches, queries_back, kvs
+    )
+    got = line.slot(
+        [grad_input, *shares], [(s, "dp", o) for s, o in zip(shares[1:], peers)], lambda: up[2]
+    )
+    share = sum(got, shares[0])
+    share_half = cuts[-1] // 2
+
+    def with_share(block, which):
+        own = lax.dynamic_slice_in_dim(share, which * share_half, share_half, 1).astype(BF)
+        below = tile_rows - part
+        own = jnp.pad(own, ((0, below - 1), (0, width // 2 - share_half)))
+        return jnp.concatenate([block, own], 0)
+
+    query_keep, query_send = with_share(query_keep, parity), with_share(query_send, 1 - parity)
+    (got,) = line.slot([out_keep, out_send], [(out_send, "ctx", 1)], lambda: up[3])
+    out_block = (out_keep.astype(F32) + got.astype(F32)).astype(BF)
+
+    def sides(first):
+        numbers = range(first, first + TILES)
+        return [[line.final[i] for i in numbers], [line.exchanged(i) for i in numbers]]
+
+    full = {}
+
+    def join_next():
+        first = len(full) * TILES
+        if len(full) == 3 or line.exchanged(first + TILES - 1) is None:
+            return []
+        full[len(full)] = join(at, *line.after(sides(first)))
+        return [full[len(full) - 1]]
+
+    joined = join_next()
+    (got,) = line.slot([query_keep, query_send], [(query_send, "ctx", 1)], lambda: out_block)
+    query_block = (query_keep.astype(F32) + got.astype(F32)).astype(BF)
+    (mlp_got,) = line.slot([*joined, mlp_sent], [(mlp_sent, "dp", far)], lambda: query_block)
+    layer_out = (line.after(middle) + mlp_partial[:rows] + mlp_got.astype(F32)).astype(BF)
+    layer_out = layer_out.reshape(tokens.shape)
+    last = 3 * TILES + 1
+
+    def both(block, mine, theirs):
+        mine, theirs = mine.astype(F32), theirs.astype(F32)
+        return jnp.where(parity == 0, mine, theirs), jnp.where(parity == 0, theirs, mine)
+
+    while last not in line.other:
+        beside = [] if line.number != 3 * TILES + 1 else [layer_out]
+        beside += join_next()
+        if line.moves:
+            line.slot(beside=beside)
+        else:
+            line.settle()
+    while len(full) < 3:
+        join_next()
+    grad_w_down, grad_w_gate, grad_w_up = [full[i] for i in range(3)]
+    pairs = [both(b, line.final[b], line.other[b]) for b in (last - 1, last)]
+    grad_w_out = jnp.concatenate([p[:part] for p in pairs[0]], 1)
+    grad_w_query = jnp.concatenate([p[:part] for p in pairs[1]], 1)
+    share = jnp.concatenate([p[part : part + 1, :share_half] for p in pairs[1]], 1)
+    pieces = width // 2 // kv_width
+    kv_rows = part // pieces
+    grad_w_kv = [
+        jnp.concatenate(
+            [p[part : part + kv_rows, j * kv_width : (j + 1) * kv_width] for j in range(pieces)], 0
+        )
+        for p in pairs[0]
     ]
-    paired = [(keep + swap(send, "ctx", 1).astype(F32)).astype(BF) for keep, send in halves]
-
-    own, other = ctx_sums(list(part_down) + list(part_gate) + list(part_up) + paired)
-    grad_w_down = join(at, own[:tiles], other[:tiles])
-    grad_w_gate = join(at, own[tiles : 2 * tiles], other[tiles : 2 * tiles]).T
-    grad_w_up = join(at, own[2 * tiles : 3 * tiles], other[2 * tiles : 3 * tiles]).T
-
-    def joined(index):
-        mine, theirs = own[index].astype(F32), other[index].astype(F32)
-        low = jnp.where(parity == 0, mine, theirs)
-        high = jnp.where(parity == 0, theirs, mine)
-        return jnp.concatenate([low, high], 1)
-
-    grad_w_out, grad_w_query, grad_w_kv = [joined(3 * tiles + i) for i in range(3)]
-
-    vectors = [
-        v.reshape(n_dp, -1)
-        for v in (
-            grad_gain_a,
-            grad_gain_m,
-            grad_bias[:, :width],
-            grad_bias[:, width : width + kv_width],
-            grad_bias[:, width + kv_width :],
-        )
-    ]
-    vectors = jnp.concatenate(vectors, 1)
-    order = [lax.dynamic_slice_in_dim(vectors, at[2 + p], 1, 0) for p in range(n_dp)]
-    step = 1
-    while step < n_dp:
-        keep, send = order[: len(order) // 2], order[len(order) // 2 :]
-        got = swap(jnp.concatenate(send, 0), "dp", step)
-        order = [k + got[i : i + 1] for i, k in enumerate(keep)]
-        step *= 2
-    share = order[0]
-    step = 1
-    while step < n_ctx:
-        share = share + swap(share, "ctx", step)
-        step *= 2
+    grad_w_kv = jnp.concatenate(grad_w_kv, 1)
+
     shares = [share[0, a:b] for a, b in zip(cuts[:-1], cuts[1:])]
     return (
         layer_out,
@@ -698,8 +962,8 @@
         shares[4],
         grad_w_out,
         shares[1],
-        grad_w_gate,
-        grad_w_up,
+        grad_w_gate.T,
+        grad_w_up.T,
         grad_w_down,
     )
 

time: 900 us -> 761 us (0.85)
  waiting for transfers between devices: 431 us -> 247 us
  Pallas kernels: 199 us -> 311 us
  matrix products: 31.7 us -> 0 us
  other arithmetic: 67.7 us -> 36.6 us
    ppermute x29 -> x32, waiting for transfers between devices: 250 us -> 78.7 us  [send(): lax.ppermute(value, 'ctx', [(2 * i + y, 2 * j + y) for i, j in pairs for...]
    pallas_call x20 -> x36, Pallas kernels: 199 us -> 311 us  [call(): pl.pallas_call(kernel, grid=grid, in_specs=specs, out_specs=out_specs, ou...]
    dot_general x3 -> x0, matrix products: 31.7 us -> none  [matmul(): lax.dot_general(left, right, (((left_dim,), (right_dim,)), ((), ())), pre...]
    select_n x22 -> x3, other arithmetic: 28.2 us -> 1.69 us  [the longest x1 1.15 us: shards(): jnp.where(turn_of == 0, half_x, half_z)]
    ppermute x62 -> x63, waiting for transfers between devices: 181 us -> 163 us  [swap(): return lax.ppermute(value, axis, [(i, i ^ offset) for i in range(size)])]
    convert_element_type x21 -> x6, other arithmetic: 27.4 us -> 9.46 us  [the longest x1 2.85 us: shards(): (line.after(middle) + mlp_partial[:rows] + mlp_got.astype(F32)).astype(BF)]
    ppermute x62 -> x63, starting transfers between devices: 41.9 us -> 50.1 us  [swap(): return lax.ppermute(value, axis, [(i, i ^ offset) for i in range(size)])]
    ppermute x29 -> x32, starting transfers between devices: 62.9 us -> 58.5 us  [send(): lax.ppermute(value, 'ctx', [(2 * i + y, 2 * j + y) for i, j in pairs for...]
  transfers between devices with their start and end apart: 93 -> 97, of which waited for: 35 -> 48; matrix products, arithmetic and copies ran while one was open for 12% -> 6% of each run, Pallas kernels for 18% -> 36%
where the time goes in v2:
time: 761 us; the launch traced here: 755 us
  Pallas kernels  311 us (41%)
  waiting for transfers between devices  247 us (32%)
  starting transfers between devices  109 us (14%)
  other arithmetic  36.6 us (5%)
  local copies, waits for them, and re-layouts  36.3 us (5%)
  between operations  15.2 us (2%)
    pallas_call x36, Pallas kernels, call(): pl.pallas_call(kernel, grid=grid, in_specs=specs, out_specs=out_specs, ou...  311 us
    ppermute x63, waiting for transfers between devices, swap(): return lax.ppermute(value, axis, [(i, i ^ offset) for i in range(size)])  163 us
    ppermute x32, waiting for transfers between devices, send(): lax.ppermute(value, 'ctx', [(2 * i + y, 2 * j + y) for i, j in pairs for...  78.7 us
    ppermute x32, starting transfers between devices, send(): lax.ppermute(value, 'ctx', [(2 * i + y, 2 * j + y) for i, j in pairs for...  58.5 us
    ppermute x63, starting transfers between devices, swap(): return lax.ppermute(value, axis, [(i, i ^ offset) for i in range(size)])  50.1 us
  transfers between devices with their start and end apart: 97, of which 48 were waited for; matrix products, arithmetic and copies ran while one was open for 6% of the time, Pallas kernels for 36%

profile of v2, /device:TPU:8, one launch (start us, length us, event | category | flops | bytes accessed | tf_op | source)
XLA Modules:
  0.0 755.0 jit_solution(7153432713563765085)
XLA Ops:
  50.5 20.3 %collective-permute-done.9 = bf16[384,768]{1,0:T(8,128)(2,1)S(1)} collective-permute-done((bf16[384,768]{1,0:T(8,128)(2,1)}, bf16[384,768]{1,0:T(8,128)(2,1)S(1)}, u32[]{:S(2)}, u32[]{:S(2)}) %collective-permute-start.9) | collective-permute-done | bytes 589856 | tf_op jit(solution)/shard_map/ppermute | solution.py:505
  84.3 18.8 %collective-permute-done.14.refs_5_.refs_7_ = bf16[256,1536]{1,0:T(8,128)(2,1)} collective-permute-done((bf16[256,1536]{1,0:T(8,128)(2,1)}, bf16[256,1536]{1,0:T(8,128)(2,1)}, u32[]{:S(2)}, u32[]{:S(2)}) %collective-permute-start.14) | collective-permute-done | bytes 786464 | tf_op jit(solution)/shard_map/ppermute | solution.py:505
  106.2 11.5 %attend_forward.1.attn = bf16[256,1536]{1,0:T(8,128)(2,1)} custom-call(bf16[256,1536]{1,0:T(8,128)(2,1)} %query.1.q_ref, bf16[8,2,2,128,256]{4,3,2,1,0:T(8,128)(2,1)} %bitcast.54, s32[128,1]{1,0:T(8,128)} %copy.36.qpos, s32[1,1024]{1,0:T(1,128)} %fusion.7.kpos), custom_call_target="tpu_custom_call" | custom-call | flops 1610612736 | bytes 3674624 | tf_op jit(solution)/shard_map/attend_forward/pallas_call | solution.py:63
  126.9 19.8 %hidden_back.1.gh = bf16[2240,2048]{1,0:T(8,128)(2,1)} custom-call(bf16[2240,1536]{1,0:T(8,128)(2,1)} %refs_1_.1, bf16[256,1536]{1,0:T(8,128)(2,1)} %bitcast.6.refs_0_.refs_2_.top, bf16[256,1536]{1,0:T(8,128)(2,1)} %collective-permute-done.10.refs_1_.refs_3_, bf16[256,1536]{1,0:T(8,128)(2,1)} %collective-permute-done.15.refs_2_.refs_4_, ...), custom_call_target="tpu_custom_call" | custom-call | flops 14092861440 | bytes 22347776 | tf_op jit(solution)/shard_map/hidden_back/pallas_call | solution.py:63
  150.1 22.1 %units.2 = (bf16[2240,1024]{1,0:T(8,128)(2,1)}, bf16[2240,1024]{1,0:T(8,128)(2,1)}, bf16[2240,1024]{1,0:T(8,128)(2,1)}) custom-call(bf16[2240,2048]{1,0:T(8,128)(2,1)} %hidden_back.1.gh, bf16[2240,1536]{1,0:T(8,128)(2,1)} %bitcast.48, bf16[2240,1536]{1,0:T(8,128)(2,1)} %bitcast.51, bf16[256,1536]{1,0:T(8,128)(2,1)} %get-tuple-element.417.refs_0_.refs_2_, ...), custom_call_target="tpu_custom_call" | custom-call | flops 14092861440 | bytes 39845888 | tf_op jit(solution)/shard_map/units/pallas_call | solution.py:63
  175.6 21.9 %units.3 = (bf16[2240,1024]{1,0:T(8,128)(2,1)}, bf16[2240,1024]{1,0:T(8,128)(2,1)}, bf16[2240,1024]{1,0:T(8,128)(2,1)}) custom-call(bf16[2240,2048]{1,0:T(8,128)(2,1)} %hidden_back.1.gh, bf16[2240,1536]{1,0:T(8,128)(2,1)} %bitcast.49, bf16[2240,1536]{1,0:T(8,128)(2,1)} %bitcast.52, bf16[256,1536]{1,0:T(8,128)(2,1)} %copy-done.65, ...), custom_call_target="tpu_custom_call" | custom-call | flops 14092861440 | bytes 39845888 | tf_op jit(solution)/shard_map/units/pallas_call | solution.py:63
  197.5 14.2 %weight_tiles.3 = (bf16[560,768]{1,0:T(8,128)(2,1)}, bf16[560,768]{1,0:T(8,128)(2,1)}, bf16[560,768]{1,0:T(8,128)(2,1)}, bf16[560,768]{1,0:T(8,128)(2,1)}) custom-call(s32[6]{0:T(128)} %stack.26.at, bf16[2240,1024]{1,0:T(8,128)(2,1)} %get-tuple-element.527.refs_0_, bf16[2240,1024]{1,0:T(8,128)(2,1)} %get-tuple-element.428.refs_1_, ...), custom_call_target="tpu_custom_call" | custom-call | flops 7046430720 | bytes 18907160 | tf_op jit(solution)/shard_map/weight_tiles/pallas_call | solution.py:63
  215.3 25.3 %rows_back.2 = (f32[512,1536]{1,0:T(8,128)}, bf16[512,1536]{1,0:T(8,128)(2,1)}) custom-call(bf16[2240,1024]{1,0:T(8,128)(2,1)} %get-tuple-element.469.refs_0_, bf16[2240,1024]{1,0:T(8,128)(2,1)} %get-tuple-element.511.refs_1_.refs_0_, bf16[2240,1536]{1,0:T(8,128)(2,1)} %bitcast.50, bf16[2240,1536]{1,0:T(8,128)(2,1)} %bitcast.53), custom_call_target="tpu_custom_call" | custom-call | flops 14092861440 | bytes 27656192 | tf_op jit(solution)/shard_map/rows_back/pallas_call | solution.py:63
  254.1 11.1 %collective-permute-done.31 = bf16[560,768]{1,0:T(8,128)(2,1)S(1)} collective-permute-done((bf16[560,768]{1,0:T(8,128)(2,1)S(1)}, bf16[560,768]{1,0:T(8,128)(2,1)S(1)}, u32[]{:S(2)}, u32[]{:S(2)}) %collective-permute-start.31) | collective-permute-done | bytes 860192 | tf_op jit(solution)/shard_map/ppermute | solution.py:545
  277.2 13.7 %weight_tiles.4 = (bf16[560,768]{1,0:T(8,128)(2,1)}, bf16[560,768]{1,0:T(8,128)(2,1)}, bf16[560,768]{1,0:T(8,128)(2,1)}, bf16[560,768]{1,0:T(8,128)(2,1)}) custom-call(s32[6]{0:T(128)} %stack.26.at, bf16[2240,1024]{1,0:T(8,128)(2,1)} %get-tuple-element.469.refs_0_, bf16[2240,1024]{1,0:T(8,128)(2,1)} %get-tuple-element.470.refs_1_, ...), custom_call_target="tpu_custom_call" | custom-call | flops 7046430720 | bytes 18907160 | tf_op jit(solution)/shard_map/weight_tiles/pallas_call | solution.py:63
  312.9 14.9 %attend_backward.1 = (bf16[256,1536]{1,0:T(8,128)(2,1)}, bf16[8,2,2,128,256]{4,3,2,1,0:T(8,128)(2,1)}) custom-call(bf16[256,1536]{1,0:T(8,128)(2,1)} %query.1.q_ref, bf16[8,2,2,128,256]{4,3,2,1,0:T(8,128)(2,1)} %bitcast.55, bf16[256,1536]{1,0:T(8,128)(2,1)} %get-tuple-element.484.go_ref, s32[128,1]{1,0:T(8,128)} %copy.36.qpos, s32[1,1024]{1,0:T(1,128)} %fusion.7.kpos, ...), custom_call_target="tpu_custom_call" | custom-call | flops 4026531840 | bytes 6689280 | tf_op jit(solution)/shard_map/attend_backward/pallas_call | solution.py:63
  339.4 11.1 %collective-permute-done.43 = bf16[256,1536]{1,0:T(8,128)(2,1)} collective-permute-done((bf16[256,1536]{1,0:T(8,128)(2,1)S(1)}, bf16[256,1536]{1,0:T(8,128)(2,1)}, u32[]{:S(2)}, u32[]{:S(2)}) %collective-permute-start.43) | collective-permute-done | bytes 786464 | tf_op jit(solution)/shard_map/ppermute | solution.py:505
  363.5 13.8 %weight_tiles.5 = (bf16[560,768]{1,0:T(8,128)(2,1)}, bf16[560,768]{1,0:T(8,128)(2,1)}, bf16[560,768]{1,0:T(8,128)(2,1)}, bf16[560,768]{1,0:T(8,128)(2,1)}) custom-call(s32[6]{0:T(128)} %stack.26.at, bf16[2240,1024]{1,0:T(8,128)(2,1)} %get-tuple-element.511.refs_1_.refs_0_, bf16[2240,1024]{1,0:T(8,128)(2,1)} %get-tuple-element.512.refs_1_, ...), custom_call_target="tpu_custom_call" | custom-call | flops 7046430720 | bytes 18907160 | tf_op jit(solution)/shard_map/weight_tiles/pallas_call | solution.py:63
  377.3 12.6 %collective-permute-done.44.arrived = bf16[560,768]{1,0:T(8,128)(2,1)S(1)} collective-permute-done((bf16[560,768]{1,0:T(8,128)(2,1)S(1)}, bf16[560,768]{1,0:T(8,128)(2,1)S(1)}, u32[]{:S(2)}, u32[]{:S(2)}) %collective-permute-start.44) | collective-permute-done | bytes 860192 | tf_op jit(solution)/shard_map/ppermute | solution.py:545
  405.1 16.3 %rows_back.3 = (f32[512,1536]{1,0:T(8,128)}, bf16[512,1536]{1,0:T(8,128)(2,1)}) custom-call(bf16[2240,1024]{1,0:T(8,128)(2,1)} %get-tuple-element.527.refs_0_, bf16[2240,1536]{1,0:T(8,128)(2,1)} %refs_1_.1), custom_call_target="tpu_custom_call" | custom-call | flops 7046430720 | bytes 16187392 | tf_op jit(solution)/shard_map/rows_back/pallas_call | solution.py:63
  484.2 7.9 %attention_weights.1 = (bf16[560,768]{1,0:T(8,128)(2,1)}, bf16[384,768]{1,0:T(8,128)(2,1)}, bf16[560,768]{1,0:T(8,128)(2,1)}, bf16[384,768]{1,0:T(8,128)(2,1)}) custom-call(s32[6]{0:T(128)} %stack.26.at, bf16[1024,384]{1,0:T(8,128)(2,1)} %get-tuple-element.756.attn, bf16[1024,384]{1,0:T(8,128)(2,1)} %get-tuple-element.757.normed, ...), custom_call_target="tpu_custom_call" | custom-call | flops 4227858432 | bytes 11812888 | tf_op jit(solution)/shard_map/attention_weights/pallas_call | solution.py:63
  525.9 16.2 %collective-permute-done.71 = bf16[560,768]{1,0:T(8,128)(2,1)S(1)} collective-permute-done((bf16[560,768]{1,0:T(8,128)(2,1)}, bf16[560,768]{1,0:T(8,128)(2,1)S(1)}, u32[]{:S(2)}, u32[]{:S(2)}) %collective-permute-start.71) | collective-permute-done | bytes 860192 | tf_op jit(solution)/shard_map/ppermute | solution.py:505
  557.2 8.4 %join.3 = f32[2240,1536]{1,0:T(8,128)} custom-call(s32[6]{0:T(128)} %stack.26.at, bf16[560,768]{1,0:T(8,128)(2,1)} %get-tuple-element.622.refs_0_, bf16[560,768]{1,0:T(8,128)(2,1)} %get-tuple-element.623.refs_1_, bf16[560,768]{1,0:T(8,128)(2,1)} %get-tuple-element.624.refs_2_, bf16[560,768]{1,0:T(8,128)(2,1)} %get-tuple-element.625.refs_3_, ...), custom_call_target="tpu_custom_call" | custom-call | bytes 20643864 | tf_op jit(solution)/shard_map/join/pallas_call | solution.py:63
  567.5 15.2 %collective-permute-done.75 = bf16[560,768]{1,0:T(8,128)(2,1)} collective-permute-done((bf16[560,768]{1,0:T(8,128)(2,1)}, bf16[560,768]{1,0:T(8,128)(2,1)}, u32[]{:S(2)}, u32[]{:S(2)}) %collective-permute-start.75) | collective-permute-done | bytes 860192 | tf_op jit(solution)/shard_map/ppermute | solution.py:505
  593.3 9.1 %collective-permute-done.79 = bf16[256,1536]{1,0:T(8,128)(2,1)} collective-permute-done((bf16[256,1536]{1,0:T(8,128)(2,1)}, bf16[256,1536]{1,0:T(8,128)(2,1)}, u32[]{:S(2)}, u32[]{:S(2)}) %collective-permute-start.79) | collective-permute-done | bytes 786464 | tf_op jit(solution)/shard_map/ppermute | solution.py:505
  634.1 8.5 %join.4 = f32[2240,1536]{1,0:T(8,128)} custom-call(s32[6]{0:T(128)} %stack.26.at, bf16[560,768]{1,0:T(8,128)(2,1)} %get-tuple-element.663.refs_0_, bf16[560,768]{1,0:T(8,128)(2,1)} %get-tuple-element.664.refs_1_, bf16[560,768]{1,0:T(8,128)(2,1)} %get-tuple-element.665.refs_2_, bf16[560,768]{1,0:T(8,128)(2,1)} %get-tuple-element.666.refs_3_, ...), custom_call_target="tpu_custom_call" | custom-call | bytes 20643864 | tf_op jit(solution)/shard_map/join/pallas_call | solution.py:63
  673.9 8.5 %collective-permute-done.89.fresh.went.arrived.across = bf16[560,768]{1,0:T(8,128)(2,1)S(1)} collective-permute-done((bf16[560,768]{1,0:T(8,128)(2,1)}, bf16[560,768]{1,0:T(8,128)(2,1)S(1)}, u32[]{:S(2)}, u32[]{:S(2)}) %collective-permute-start.89) | collective-permute-done | bytes 860192 | tf_op jit(solution)/shard_map/ppermute | solution.py:545
  697.3 10.9 %collective-permute-done.92.refs_7_ = bf16[560,768]{1,0:T(8,128)(2,1)S(1)} collective-permute-done((bf16[560,768]{1,0:T(8,128)(2,1)}, bf16[560,768]{1,0:T(8,128)(2,1)S(1)}, u32[]{:S(2)}, u32[]{:S(2)}) %collective-permute-start.92) | collective-permute-done | bytes 860192 | tf_op jit(solution)/shard_map/ppermute | solution.py:505
  715.3 8.5 %join.5 = f32[2240,1536]{1,0:T(8,128)} custom-call(s32[6]{0:T(128)} %stack.26.at, bf16[560,768]{1,0:T(8,128)(2,1)} %get-tuple-element.705.refs_0_, bf16[560,768]{1,0:T(8,128)(2,1)} %get-tuple-element.706.refs_1_, bf16[560,768]{1,0:T(8,128)(2,1)} %get-tuple-element.707.refs_2_, bf16[560,768]{1,0:T(8,128)(2,1)} %get-tuple-element.708.refs_3_, ...), custom_call_target="tpu_custom_call" | custom-call | bytes 20643864 | tf_op jit(solution)/shard_map/join/pallas_call | solution.py:63
  (430 shorter events, 399.1 us)
Async XLA Ops:
  7.2 99.0 %all-gather.3.cloned.1.call-start = ((), (), s32[]{:S(2)}) async-start(), calls=%async_computation.2 | async-start | bytes 2359296 | tf_op jit(solution)/shard_map/all_gather | solution.py:730
  39.8 397.0 %reduce-scatter.2.cloned.1.call-start = ((), (), s32[]{:S(2)}) async-start(), calls=%async_computation.1 | async-start | bytes 2359296 | tf_op jit(solution)/shard_map/reduce_scatter | solution.py:831
  73.7 29.4 %collective-permute-start.12 = (bf16[384,1536]{1,0:T(8,128)(2,1)S(1)}, bf16[384,1536]{1,0:T(8,128)(2,1)S(1)}, u32[]{:S(2)}, u32[]{:S(2)}) collective-permute-start(bf16[384,1536]{1,0:T(8,128)(2,1)S(1)} %copy-done.6), channel_id=1, source_target_pairs={{0,2},{1,3},{2,0},{3,1},{4,6},{5,7},{6,4},{7,5},{8,10},{9,11},{10,... | collective-permute-start | bytes 3538952 | tf_op jit(solution)/shard_map/ppermute | solution.py:505
  75.4 27.7 %collective-permute-start.13 = (bf16[384,1536]{1,0:T(8,128)(2,1)S(1)}, bf16[384,1536]{1,0:T(8,128)(2,1)}, u32[]{:S(2)}, u32[]{:S(2)}) collective-permute-start(bf16[384,1536]{1,0:T(8,128)(2,1)S(1)} %copy-done.6), channel_id=1, source_target_pairs={{0,1},{1,0},{2,3},{3,2},{4,5},{5,4},{6,7},{7,6},{8,9},{9,8},{10,11... | collective-permute-start | bytes 3538952 | tf_op jit(solution)/shard_map/ppermute | solution.py:505
  75.4 27.7 %collective-permute-start.14 = (bf16[256,1536]{1,0:T(8,128)(2,1)}, bf16[256,1536]{1,0:T(8,128)(2,1)}, u32[]{:S(2)}, u32[]{:S(2)}) collective-permute-start(bf16[256,1536]{1,0:T(8,128)(2,1)} %collective-permute-done.10.refs_1_.refs_3_), channel_id=1, source_target_pairs={{0,4},{4,0},{8,12},{12,8},{16,20},{20,16},{24,28},{28,24},{1,5},{5... | collective-permute-start | bytes 2359304 | tf_op jit(solution)/shard_map/ppermute | solution.py:505
  76.9 26.2 %collective-permute-start.15 = (bf16[256,1536]{1,0:T(8,128)(2,1)}, bf16[256,1536]{1,0:T(8,128)(2,1)}, u32[]{:S(2)}, u32[]{:S(2)}) collective-permute-start(bf16[256,1536]{1,0:T(8,128)(2,1)} %bitcast.6.refs_0_.refs_2_.top), channel_id=1, source_target_pairs={{0,1},{1,0},{2,3},{3,2},{4,5},{5,4},{6,7},{7,6},{8,9},{9,8},{10,11... | collective-permute-start | bytes 2359304 | tf_op jit(solution)/shard_map/ppermute | solution.py:505
  211.8 28.8 %collective-permute-start.27 = (bf16[560,768]{1,0:T(8,128)(2,1)}, bf16[560,768]{1,0:T(8,128)(2,1)S(1)}, u32[]{:S(2)}, u32[]{:S(2)}) collective-permute-start(bf16[560,768]{1,0:T(8,128)(2,1)} %get-tuple-element.433), channel_id=1, source_target_pairs={{0,8},{4,12},{24,16},{28,20},{1,9},{5,13},{25,17},{29,21},{2,10},{... | collective-permute-start | bytes 2580488 | tf_op jit(solution)/shard_map/ppermute | solution.py:545
  213.1 27.5 %collective-permute-start.28 = (bf16[256,384]{1,0:T(8,128)(2,1)}, bf16[256,384]{1,0:T(8,128)(2,1)S(1)}, u32[]{:S(2)}, u32[]{:S(2)}) collective-permute-start(bf16[256,384]{1,0:T(8,128)(2,1)} %get-tuple-element.434), channel_id=1, source_target_pairs={{0,2},{1,3},{2,0},{3,1},{4,6},{5,7},{6,4},{7,5},{8,10},{9,11},{10,... | collective-permute-start | bytes 589832 | tf_op jit(solution)/shard_map/ppermute | solution.py:505
  214.5 26.1 %collective-permute-start.29 = (bf16[256,384]{1,0:T(8,128)(2,1)}, bf16[256,384]{1,0:T(8,128)(2,1)S(1)}, u32[]{:S(2)}, u32[]{:S(2)}) collective-permute-start(bf16[256,384]{1,0:T(8,128)(2,1)} %get-tuple-element.435), channel_id=1, source_target_pairs={{0,1},{1,0},{2,3},{3,2},{4,5},{5,4},{6,7},{7,6},{8,9},{9,8},{10,11... | collective-permute-start | bytes 589832 | tf_op jit(solution)/shard_map/ppermute | solution.py:505
  214.5 26.1 %collective-permute-start.30 = (bf16[256,384]{1,0:T(8,128)(2,1)S(1)}, bf16[256,384]{1,0:T(8,128)(2,1)S(1)}, u32[]{:S(2)}, u32[]{:S(2)}) collective-permute-start(bf16[256,384]{1,0:T(8,128)(2,1)S(1)} %get-tuple-element.436), channel_id=1, source_target_pairs={{0,3},{1,2},{2,1},{3,0},{4,7},{5,6},{6,5},{7,4},{8,11},{9,10},{10,... | collective-permute-start | bytes 589832 | tf_op jit(solution)/shard_map/ppermute | solution.py:505
  241.4 24.7 %collective-permute-start.32 = (bf16[512,1536]{1,0:T(8,128)(2,1)}, bf16[512,1536]{1,0:T(8,128)(2,1)}, u32[]{:S(2)}, u32[]{:S(2)}) collective-permute-start(bf16[512,1536]{1,0:T(8,128)(2,1)} %get-tuple-element.449), channel_id=1, source_target_pairs={{0,1},{1,0},{2,3},{3,2},{4,5},{5,4},{6,7},{7,6},{8,9},{9,8},{10,11... | collective-permute-start | bytes 4718600 | tf_op jit(solution)/shard_map/ppermute | solution.py:505
  294.4 33.3 %collective-permute-start.39 = (bf16[560,768]{1,0:T(8,128)(2,1)}, bf16[560,768]{1,0:T(8,128)(2,1)}, u32[]{:S(2)}, u32[]{:S(2)}) collective-permute-start(bf16[560,768]{1,0:T(8,128)(2,1)} %get-tuple-element.475.went.sent), channel_id=1, source_target_pairs={{0,8},{4,12},{24,16},{28,20},{1,9},{5,13},{25,17},{29,21},{2,10},{... | collective-permute-start | bytes 2580488 | tf_op jit(solution)/shard_map/ppermute | solution.py:545
  295.7 32.1 %collective-permute-start.40 = (bf16[560,768]{1,0:T(8,128)(2,1)}, bf16[560,768]{1,0:T(8,128)(2,1)}, u32[]{:S(2)}, u32[]{:S(2)}) collective-permute-start(bf16[560,768]{1,0:T(8,128)(2,1)} %add_convert_fusion.2.summed), channel_id=1, source_target_pairs={{8,16},{12,20},{16,8},{20,12},{9,17},{13,21},{17,9},{21,13},{10,18... | collective-permute-start | bytes 2580488 | tf_op jit(solution)/shard_map/ppermute | solution.py:545
  353.7 40.5 %collective-permute-start.47 = (bf16[512,1536]{1,0:T(8,128)(2,1)}, bf16[512,1536]{1,0:T(8,128)(2,1)}, u32[]{:S(2)}, u32[]{:S(2)}) collective-permute-start(bf16[512,1536]{1,0:T(8,128)(2,1)} %constant_dynamic-update-slice_fusion.2.refs_0_), channel_id=1, source_target_pairs={{0,1},{1,0},{2,3},{3,2},{4,5},{5,4},{6,7},{7,6},{8,9},{9,8},{10,11... | collective-permute-start | bytes 4718600 | tf_op jit(solution)/shard_map/ppermute | solution.py:505
  353.7 36.1 %collective-permute-start.44 = (bf16[560,768]{1,0:T(8,128)(2,1)S(1)}, bf16[560,768]{1,0:T(8,128)(2,1)S(1)}, u32[]{:S(2)}, u32[]{:S(2)}) collective-permute-start(bf16[560,768]{1,0:T(8,128)(2,1)S(1)} %copy-done.32), channel_id=1, source_target_pairs={{0,8},{4,12},{24,16},{28,20},{8,0},{12,4},{16,24},{20,28},{1,9},{5... | collective-permute-start | bytes 2580488 | tf_op jit(solution)/shard_map/ppermute | solution.py:545
  353.8 40.4 %collective-permute-start.45 = (bf16[560,768]{1,0:T(8,128)(2,1)S(1)}, bf16[560,768]{1,0:T(8,128)(2,1)}, u32[]{:S(2)}, u32[]{:S(2)}) collective-permute-start(bf16[560,768]{1,0:T(8,128)(2,1)S(1)} %copy-done.31), channel_id=1, source_target_pairs={{8,16},{12,20},{16,8},{20,12},{9,17},{13,21},{17,9},{21,13},{10,18... | collective-permute-start | bytes 2580488 | tf_op jit(solution)/shard_map/ppermute | solution.py:545
  396.3 28.3 %collective-permute-start.51 = (bf16[512,1536]{1,0:T(8,128)(2,1)}, bf16[512,1536]{1,0:T(8,128)(2,1)}, u32[]{:S(2)}, u32[]{:S(2)}) collective-permute-start(bf16[512,1536]{1,0:T(8,128)(2,1)} %constant_dynamic-update-slice_fusion.4.refs_2_), channel_id=1, source_target_pairs={{0,1},{1,0},{2,3},{3,2},{4,5},{5,4},{6,7},{7,6},{8,9},{9,8},{10,11... | collective-permute-start | bytes 4718600 | tf_op jit(solution)/shard_map/ppermute | solution.py:505
  396.3 25.1 %collective-permute-start.48 = (bf16[560,768]{1,0:T(8,128)(2,1)}, bf16[560,768]{1,0:T(8,128)(2,1)S(1)}, u32[]{:S(2)}, u32[]{:S(2)}) collective-permute-start(bf16[560,768]{1,0:T(8,128)(2,1)} %get-tuple-element.517.sent), channel_id=1, source_target_pairs={{0,8},{4,12},{24,16},{28,20},{8,0},{12,4},{16,24},{20,28},{1,9},{5... | collective-permute-start | bytes 2580488 | tf_op jit(solution)/shard_map/ppermute | solution.py:545
  396.3 25.1 %collective-permute-start.49 = (bf16[560,768]{1,0:T(8,128)(2,1)}, bf16[560,768]{1,0:T(8,128)(2,1)}, u32[]{:S(2)}, u32[]{:S(2)}) collective-permute-start(bf16[560,768]{1,0:T(8,128)(2,1)} %get-tuple-element.518.summed), channel_id=1, source_target_pairs={{8,16},{12,20},{16,8},{20,12},{9,17},{13,21},{17,9},{21,13},{10,18... | collective-permute-start | bytes 2580488 | tf_op jit(solution)/shard_map/ppermute | solution.py:545
  398.9 25.8 %collective-permute-start.50 = (bf16[560,768]{1,0:T(8,128)(2,1)}, bf16[560,768]{1,0:T(8,128)(2,1)}, u32[]{:S(2)}, u32[]{:S(2)}) collective-permute-start(bf16[560,768]{1,0:T(8,128)(2,1)} %get-tuple-element.622.refs_0_), channel_id=1, source_target_pairs={{0,4},{4,0},{8,12},{12,8},{16,20},{20,16},{24,28},{28,24},{1,5},{5... | collective-permute-start | bytes 2580488 | tf_op jit(solution)/shard_map/ppermute | solution.py:505
  424.6 27.0 %collective-permute-start.55 = (bf16[512,1536]{1,0:T(8,128)(2,1)}, bf16[512,1536]{1,0:T(8,128)(2,1)S(1)}, u32[]{:S(2)}, u32[]{:S(2)}) collective-permute-start(bf16[512,1536]{1,0:T(8,128)(2,1)} %get-tuple-element.537), channel_id=1, source_target_pairs={{0,1},{1,0},{2,3},{3,2},{4,5},{5,4},{6,7},{7,6},{8,9},{9,8},{10,11... | collective-permute-start | bytes 4718600 | tf_op jit(solution)/shard_map/ppermute | solution.py:505
  424.7 25.2 %collective-permute-start.52 = (bf16[560,768]{1,0:T(8,128)(2,1)S(1)}, bf16[560,768]{1,0:T(8,128)(2,1)}, u32[]{:S(2)}, u32[]{:S(2)}) collective-permute-start(bf16[560,768]{1,0:T(8,128)(2,1)S(1)} %copy-done.29), channel_id=1, source_target_pairs={{0,8},{4,12},{24,16},{28,20},{8,0},{12,4},{16,24},{20,28},{1,9},{5... | collective-permute-start | bytes 2580488 | tf_op jit(solution)/shard_map/ppermute | solution.py:545
  504.3 37.7 %collective-permute-start.71 = (bf16[560,768]{1,0:T(8,128)(2,1)}, bf16[560,768]{1,0:T(8,128)(2,1)S(1)}, u32[]{:S(2)}, u32[]{:S(2)}) collective-permute-start(bf16[560,768]{1,0:T(8,128)(2,1)} %get-tuple-element.595), channel_id=1, source_target_pairs={{0,4},{4,0},{8,12},{12,8},{16,20},{20,16},{24,28},{28,24},{1,5},{5... | collective-permute-start | bytes 2580488 | tf_op jit(solution)/shard_map/ppermute | solution.py:505
  545.4 37.3 %collective-permute-start.75 = (bf16[560,768]{1,0:T(8,128)(2,1)}, bf16[560,768]{1,0:T(8,128)(2,1)}, u32[]{:S(2)}, u32[]{:S(2)}) collective-permute-start(bf16[560,768]{1,0:T(8,128)(2,1)} %fusion.4), channel_id=1, source_target_pairs={{0,4},{4,0},{8,12},{12,8},{16,20},{20,16},{24,28},{28,24},{1,5},{5... | collective-permute-start | bytes 2580488 | tf_op jit(solution)/shard_map/ppermute | solution.py:505
  (145 other events, 1972.8 us)
Sparse Core Ops, SparseCore 0:
  39.9 62.6 all-gather.2
  353.9 82.8 reduce-scatter.1

commit v3 on v2

--- a/solution.py
+++ b/solution.py
@@ -710,13 +710,7 @@
     ]
     bias_kv = jnp.concatenate([bias_key, bias_value], 1)
 
-    turn_of = lax.axis_index("ctx") // 2 % 2
     grad_rows = cotangent.reshape(rows, width)
-    half_query = lax.dynamic_slice_in_dim(w_query, turn_of * (width // 2), width // 2, 1)
-    half_x, top_y, query_c = swaps(
-        [(half_query, "dp", far), (grad_rows, "ctx", 1), (w_query, "dp", close)], [kv_x]
-    )
-
     inputs = tokens.reshape(rows, width)
     args = (at, inputs, gain_one, bias_kv, table, *full_kv)
     normed_one, kv_own = call(
@@ -728,9 +722,8 @@
         flops=4 * rows * width * kv_width,
     )
     kv_all = lax.all_gather(kv_own, "ctx", axis=0, tiled=False)
-    half_z, top_x = swaps([(half_x, "ctx", 2), (grad_rows, "dp", far)], [half_x])
-    query_x = jnp.concatenate(
-        [jnp.where(turn_of == 0, half_x, half_z), jnp.where(turn_of == 0, half_z, half_x)], 1
+    query_x, top_y, query_c = swaps(
+        [(w_query, "dp", far), (grad_rows, "ctx", 1), (w_query, "dp", close)], [normed_one]
     )
     (query_xc,) = swaps([(query_x, "dp", close)])
     full_query = [w_query, query_x, query_c, query_xc]
@@ -743,19 +736,18 @@
         [shape((rows, width), BF)],
         flops=2 * rows * width * width,
     )[0]
-    out_x, out_c, top_xy, top_c = swaps(
-        [(w_out, "dp", far), (w_out, "dp", close), (top_x, "ctx", 1), (grad_rows, "dp", close)],
-        [top_x],
-        [queries],
+    top_x, top_c = swaps(
+        [(grad_rows, "dp", far), (grad_rows, "dp", close)], [query_x], [queries]
     )
     attn_vec = attend_forward(queries, kv_all, qpos, kpos)
-    out_xc, top_xc, top_yc, top_xyc = swaps(
-        [(out_x, "dp", close), (top_x, "dp", close), (top_y, "dp", close), (top_xy, "dp", close)],
-        [out_x],
-        [attn_vec],
-    )
+    top_xc, top_yc = swaps([(top_x, "dp", close), (top_y, "dp", close)], [top_x], [attn_vec])
+    tops = [grad_rows, top_x, top_c, top_xc]
+    grad_hidden = hidden_back(w_down, tie(tops, attn_vec))
+    out_x, out_c, top_xy = swaps(
+        [(w_out, "dp", far), (w_out, "dp", close), (top_x, "ctx", 1)], [top_x], [grad_hidden]
+    )
+    (out_xc,) = swaps([(out_x, "dp", close)])
     full_out = [w_out, out_x, out_c, out_xc]
-    tops = [grad_rows, top_x, top_c, top_xc, top_y, top_xy, top_yc, top_xyc]
     args = (at, inputs, attn_vec, gain_two, *full_out)
     middle, normed_two = call(
         functools.partial(out_norm_kernel, n_dp),
@@ -766,12 +758,13 @@
         flops=2 * rows * width * width,
     )
 
-    tops = tie(tops, normed_two)
-    grad_hidden = hidden_back(w_down, tops)
+    (top_xyc,) = swaps([(top_xy, "dp", close)], [], [normed_two])
+    tops += [top_y, top_xy, top_yc, top_xyc]
+    grad_hidden_near = hidden_back(w_down, tie(tops[n_dp:], normed_two))
     norm_x, norm_y, norm_c = swaps(
         [(normed_two, "dp", far), (normed_two, "ctx", 1), (normed_two, "dp", close)],
         [],
-        [grad_hidden],
+        [grad_hidden_near],
     )
     (norm_xc,) = swaps([(norm_x, "dp", close)])
     wide_gate, wide_up = w_gate.T, w_up.T
@@ -794,7 +787,7 @@
             [lax.dynamic_slice_in_dim(value, dp_index * part, part, 1)] + list(got), 0
         )
 
-    near = units(grad_hidden, 1, wide_gate, wide_up, norms[n_dp:])
+    near = units(grad_hidden_near, 0, wide_gate, wide_up, norms[n_dp:])
     down = weight_tiles(at, tops, [hidden, near[0]])
     line = CtxSums(down[0])
 

time: 761 us -> 757 us (level)
  waiting for transfers between devices: 247 us -> 258 us
  starting transfers between devices: 109 us -> 101 us
    ppermute x63 -> x62, starting transfers between devices: 50.1 us -> 39.5 us  [swap(): return lax.ppermute(value, axis, [(i, i ^ offset) for i in range(size)])]
    ppermute x63 -> x62, waiting for transfers between devices: 163 us -> 169 us  [swap(): return lax.ppermute(value, axis, [(i, i ^ offset) for i in range(size)])]
    pallas_call x36 -> x37, Pallas kernels: 311 us -> 314 us  [call(): pl.pallas_call(kernel, grid=grid, in_specs=specs, out_specs=out_specs, ou...]
  transfers between devices with their start and end apart: 97 -> 96, of which waited for: 48 -> 52; matrix products, arithmetic and copies ran while one was open for 6% -> 5% of each run, Pallas kernels for 36% -> 36%
where the time goes in v3:
time: 757 us; the launch traced here: 752 us
  Pallas kernels  314 us (41%)
  waiting for transfers between devices  258 us (34%)
  starting transfers between devices  101 us (13%)
  other arithmetic  31.8 us (4%)
  local copies, waits for them, and re-layouts  30.9 us (4%)
  between operations  15.2 us (2%)
    pallas_call x37, Pallas kernels, call(): pl.pallas_call(kernel, grid=grid, in_specs=specs, out_specs=out_specs, ou...  314 us
    ppermute x62, waiting for transfers between devices, swap(): return lax.ppermute(value, axis, [(i, i ^ offset) for i in range(size)])  169 us
    ppermute x32, waiting for transfers between devices, send(): lax.ppermute(value, 'ctx', [(2 * i + y, 2 * j + y) for i, j in pairs for...  84.5 us
    ppermute x32, starting transfers between devices, send(): lax.ppermute(value, 'ctx', [(2 * i + y, 2 * j + y) for i, j in pairs for...  61.5 us
    ppermute x62, starting transfers between devices, swap(): return lax.ppermute(value, axis, [(i, i ^ offset) for i in range(size)])  39.5 us
  transfers between devices with their start and end apart: 96, of which 52 were waited for; matrix products, arithmetic and copies ran while one was open for 5% of the time, Pallas kernels for 36%

profile of v3, /device:TPU:8, one launch (start us, length us, event | category | flops | bytes accessed | tf_op | source)
XLA Modules:
  0.0 751.6 jit_solution(12758550184536838447)
XLA Ops:
  16.3 9.4 %collective-permute-done.1.refs_1_.refs_5_ = bf16[384,512]{1,0:T(8,128)(2,1)S(1)} collective-permute-done((bf16[384,512]{1,0:T(8,128)(2,1)S(1)}, bf16[384,512]{1,0:T(8,128)(2,1)S(1)}, u32[]{:S(2)}, u32[]{:S(2)}) %collective-permute-start.1) | collective-permute-done | bytes 393248 | tf_op jit(solution)/shard_map/ppermute | solution.py:505
  35.5 21.5 %collective-permute-done.7.refs_0_.refs_6_ = bf16[256,1536]{1,0:T(8,128)(2,1)S(1)} collective-permute-done((bf16[256,1536]{1,0:T(8,128)(2,1)}, bf16[256,1536]{1,0:T(8,128)(2,1)S(1)}, u32[]{:S(2)}, u32[]{:S(2)}) %collective-permute-start.7) | collective-permute-done | bytes 786464 | tf_op jit(solution)/shard_map/ppermute | solution.py:505
  71.8 10.8 %collective-permute-done.10.refs_1_.refs_3_ = bf16[256,1536]{1,0:T(8,128)(2,1)} collective-permute-done((bf16[256,1536]{1,0:T(8,128)(2,1)}, bf16[256,1536]{1,0:T(8,128)(2,1)}, u32[]{:S(2)}, u32[]{:S(2)}) %collective-permute-start.10) | collective-permute-done | bytes 786464 | tf_op jit(solution)/shard_map/ppermute | solution.py:505
  86.6 11.5 %attend_forward.1.attn = bf16[256,1536]{1,0:T(8,128)(2,1)} custom-call(bf16[256,1536]{1,0:T(8,128)(2,1)} %query.1.q_ref, bf16[8,2,2,128,256]{4,3,2,1,0:T(8,128)(2,1)} %bitcast.54, s32[128,1]{1,0:T(8,128)} %copy.36.qpos, s32[1,1024]{1,0:T(1,128)} %fusion.7.kpos), custom_call_target="tpu_custom_call" | custom-call | flops 1610612736 | bytes 3674624 | tf_op jit(solution)/shard_map/attend_forward/pallas_call | solution.py:63
  98.1 11.4 %hidden_back.2.gh = bf16[2240,1024]{1,0:T(8,128)(2,1)} custom-call(bf16[2240,1536]{1,0:T(8,128)(2,1)} %refs_1_.1, bf16[256,1536]{1,0:T(8,128)(2,1)} %bitcast.6.refs_0_.refs_2_.top, bf16[256,1536]{1,0:T(8,128)(2,1)} %collective-permute-done.10.refs_1_.refs_3_, bf16[256,1536]{1,0:T(8,128)(2,1)} %collective-permute-done.11.refs_2_.refs_4_, ...), custom_call_target="tpu_custom_call" | custom-call | flops 7046430720 | bytes 14614528 | tf_op jit(solution)/shard_map/hidden_back/pallas_call | solution.py:63
  124.0 11.4 %hidden_back.3.gh = bf16[2240,1024]{1,0:T(8,128)(2,1)} custom-call(bf16[2240,1536]{1,0:T(8,128)(2,1)} %refs_1_.1, bf16[256,1536]{1,0:T(8,128)(2,1)} %copy-done.67, bf16[256,1536]{1,0:T(8,128)(2,1)} %collective-permute-done.14.refs_1_.refs_7_, bf16[256,1536]{1,0:T(8,128)(2,1)} %collective-permute-done.16.refs_2_.refs_8_, ...), custom_call_target="tpu_custom_call" | custom-call | flops 7046430720 | bytes 14614528 | tf_op jit(solution)/shard_map/hidden_back/pallas_call | solution.py:63
  145.9 22.1 %units.2 = (bf16[2240,1024]{1,0:T(8,128)(2,1)}, bf16[2240,1024]{1,0:T(8,128)(2,1)}, bf16[2240,1024]{1,0:T(8,128)(2,1)}) custom-call(bf16[2240,1024]{1,0:T(8,128)(2,1)} %hidden_back.2.gh, bf16[2240,1536]{1,0:T(8,128)(2,1)} %bitcast.48, bf16[2240,1536]{1,0:T(8,128)(2,1)} %bitcast.51, bf16[256,1536]{1,0:T(8,128)(2,1)} %get-tuple-element.400.refs_0_.refs_2_, ...), custom_call_target="tpu_custom_call" | custom-call | flops 14092861440 | bytes 35258368 | tf_op jit(solution)/shard_map/units/pallas_call | solution.py:63
  171.5 22.0 %units.3 = (bf16[2240,1024]{1,0:T(8,128)(2,1)}, bf16[2240,1024]{1,0:T(8,128)(2,1)}, bf16[2240,1024]{1,0:T(8,128)(2,1)}) custom-call(bf16[2240,1024]{1,0:T(8,128)(2,1)} %hidden_back.3.gh, bf16[2240,1536]{1,0:T(8,128)(2,1)} %bitcast.49, bf16[2240,1536]{1,0:T(8,128)(2,1)} %bitcast.52, bf16[256,1536]{1,0:T(8,128)(2,1)} %copy-done.63, ...), custom_call_target="tpu_custom_call" | custom-call | flops 14092861440 | bytes 35258368 | tf_op jit(solution)/shard_map/units/pallas_call | solution.py:63
  193.5 14.4 %weight_tiles.3 = (bf16[560,768]{1,0:T(8,128)(2,1)}, bf16[560,768]{1,0:T(8,128)(2,1)}, bf16[560,768]{1,0:T(8,128)(2,1)}, bf16[560,768]{1,0:T(8,128)(2,1)}) custom-call(s32[6]{0:T(128)} %stack.26.at, bf16[2240,1024]{1,0:T(8,128)(2,1)} %get-tuple-element.517.refs_0_, bf16[2240,1024]{1,0:T(8,128)(2,1)} %get-tuple-element.418.refs_1_, ...), custom_call_target="tpu_custom_call" | custom-call | flops 7046430720 | bytes 18907160 | tf_op jit(solution)/shard_map/weight_tiles/pallas_call | solution.py:63
  211.4 25.2 %rows_back.2 = (f32[512,1536]{1,0:T(8,128)}, bf16[512,1536]{1,0:T(8,128)(2,1)}) custom-call(bf16[2240,1024]{1,0:T(8,128)(2,1)} %get-tuple-element.459.refs_0_, bf16[2240,1024]{1,0:T(8,128)(2,1)} %get-tuple-element.501.refs_1_.refs_0_, bf16[2240,1536]{1,0:T(8,128)(2,1)} %bitcast.50, bf16[2240,1536]{1,0:T(8,128)(2,1)} %bitcast.53), custom_call_target="tpu_custom_call" | custom-call | flops 14092861440 | bytes 27656192 | tf_op jit(solution)/shard_map/rows_back/pallas_call | solution.py:63
  250.1 11.1 %collective-permute-done.30 = bf16[560,768]{1,0:T(8,128)(2,1)S(1)} collective-permute-done((bf16[560,768]{1,0:T(8,128)(2,1)S(1)}, bf16[560,768]{1,0:T(8,128)(2,1)S(1)}, u32[]{:S(2)}, u32[]{:S(2)}) %collective-permute-start.30) | collective-permute-done | bytes 860192 | tf_op jit(solution)/shard_map/ppermute | solution.py:545
  272.7 13.8 %weight_tiles.4 = (bf16[560,768]{1,0:T(8,128)(2,1)}, bf16[560,768]{1,0:T(8,128)(2,1)}, bf16[560,768]{1,0:T(8,128)(2,1)}, bf16[560,768]{1,0:T(8,128)(2,1)}) custom-call(s32[6]{0:T(128)} %stack.26.at, bf16[2240,1024]{1,0:T(8,128)(2,1)} %get-tuple-element.459.refs_0_, bf16[2240,1024]{1,0:T(8,128)(2,1)} %get-tuple-element.460.refs_1_, ...), custom_call_target="tpu_custom_call" | custom-call | flops 7046430720 | bytes 18907160 | tf_op jit(solution)/shard_map/weight_tiles/pallas_call | solution.py:63
  309.4 14.9 %attend_backward.1 = (bf16[256,1536]{1,0:T(8,128)(2,1)}, bf16[8,2,2,128,256]{4,3,2,1,0:T(8,128)(2,1)}) custom-call(bf16[256,1536]{1,0:T(8,128)(2,1)} %query.1.q_ref, bf16[8,2,2,128,256]{4,3,2,1,0:T(8,128)(2,1)} %bitcast.55, bf16[256,1536]{1,0:T(8,128)(2,1)} %get-tuple-element.474.go_ref, s32[128,1]{1,0:T(8,128)} %copy.36.qpos, s32[1,1024]{1,0:T(1,128)} %fusion.7.kpos, ...), custom_call_target="tpu_custom_call" | custom-call | flops 4026531840 | bytes 6689280 | tf_op jit(solution)/shard_map/attend_backward/pallas_call | solution.py:63
  336.1 10.9 %collective-permute-done.42 = bf16[256,1536]{1,0:T(8,128)(2,1)} collective-permute-done((bf16[256,1536]{1,0:T(8,128)(2,1)S(1)}, bf16[256,1536]{1,0:T(8,128)(2,1)}, u32[]{:S(2)}, u32[]{:S(2)}) %collective-permute-start.42) | collective-permute-done | bytes 786464 | tf_op jit(solution)/shard_map/ppermute | solution.py:505
  359.8 13.8 %weight_tiles.5 = (bf16[560,768]{1,0:T(8,128)(2,1)}, bf16[560,768]{1,0:T(8,128)(2,1)}, bf16[560,768]{1,0:T(8,128)(2,1)}, bf16[560,768]{1,0:T(8,128)(2,1)}) custom-call(s32[6]{0:T(128)} %stack.26.at, bf16[2240,1024]{1,0:T(8,128)(2,1)} %get-tuple-element.501.refs_1_.refs_0_, bf16[2240,1024]{1,0:T(8,128)(2,1)} %get-tuple-element.502.refs_1_, ...), custom_call_target="tpu_custom_call" | custom-call | flops 7046430720 | bytes 18907160 | tf_op jit(solution)/shard_map/weight_tiles/pallas_call | solution.py:63
  373.6 13.5 %collective-permute-done.43.arrived = bf16[560,768]{1,0:T(8,128)(2,1)S(1)} collective-permute-done((bf16[560,768]{1,0:T(8,128)(2,1)S(1)}, bf16[560,768]{1,0:T(8,128)(2,1)S(1)}, u32[]{:S(2)}, u32[]{:S(2)}) %collective-permute-start.43) | collective-permute-done | bytes 860192 | tf_op jit(solution)/shard_map/ppermute | solution.py:545
  402.7 16.3 %rows_back.3 = (f32[512,1536]{1,0:T(8,128)}, bf16[512,1536]{1,0:T(8,128)(2,1)}) custom-call(bf16[2240,1024]{1,0:T(8,128)(2,1)} %get-tuple-element.517.refs_0_, bf16[2240,1536]{1,0:T(8,128)(2,1)} %refs_1_.1), custom_call_target="tpu_custom_call" | custom-call | flops 7046430720 | bytes 16187392 | tf_op jit(solution)/shard_map/rows_back/pallas_call | solution.py:63
  522.1 16.1 %collective-permute-done.70 = bf16[560,768]{1,0:T(8,128)(2,1)S(1)} collective-permute-done((bf16[560,768]{1,0:T(8,128)(2,1)}, bf16[560,768]{1,0:T(8,128)(2,1)S(1)}, u32[]{:S(2)}, u32[]{:S(2)}) %collective-permute-start.70) | collective-permute-done | bytes 860192 | tf_op jit(solution)/shard_map/ppermute | solution.py:505
  563.4 14.9 %collective-permute-done.74 = bf16[560,768]{1,0:T(8,128)(2,1)} collective-permute-done((bf16[560,768]{1,0:T(8,128)(2,1)}, bf16[560,768]{1,0:T(8,128)(2,1)}, u32[]{:S(2)}, u32[]{:S(2)}) %collective-permute-start.74) | collective-permute-done | bytes 860192 | tf_op jit(solution)/shard_map/ppermute | solution.py:505
  589.8 9.0 %collective-permute-done.78 = bf16[256,1536]{1,0:T(8,128)(2,1)} collective-permute-done((bf16[256,1536]{1,0:T(8,128)(2,1)}, bf16[256,1536]{1,0:T(8,128)(2,1)}, u32[]{:S(2)}, u32[]{:S(2)}) %collective-permute-start.78) | collective-permute-done | bytes 786464 | tf_op jit(solution)/shard_map/ppermute | solution.py:505
  630.7 8.5 %join.4 = f32[2240,1536]{1,0:T(8,128)} custom-call(s32[6]{0:T(128)} %stack.26.at, bf16[560,768]{1,0:T(8,128)(2,1)} %get-tuple-element.653.refs_0_, bf16[560,768]{1,0:T(8,128)(2,1)} %get-tuple-element.654.refs_1_, bf16[560,768]{1,0:T(8,128)(2,1)} %get-tuple-element.655.refs_2_, bf16[560,768]{1,0:T(8,128)(2,1)} %get-tuple-element.656.refs_3_, ...), custom_call_target="tpu_custom_call" | custom-call | bytes 20643864 | tf_op jit(solution)/shard_map/join/pallas_call | solution.py:63
  668.6 11.1 %collective-permute-done.88.fresh.went.arrived.across = bf16[560,768]{1,0:T(8,128)(2,1)S(1)} collective-permute-done((bf16[560,768]{1,0:T(8,128)(2,1)}, bf16[560,768]{1,0:T(8,128)(2,1)S(1)}, u32[]{:S(2)}, u32[]{:S(2)}) %collective-permute-start.88) | collective-permute-done | bytes 860192 | tf_op jit(solution)/shard_map/ppermute | solution.py:545
  694.6 10.8 %collective-permute-done.91.refs_7_ = bf16[560,768]{1,0:T(8,128)(2,1)S(1)} collective-permute-done((bf16[560,768]{1,0:T(8,128)(2,1)}, bf16[560,768]{1,0:T(8,128)(2,1)S(1)}, u32[]{:S(2)}, u32[]{:S(2)}) %collective-permute-start.91) | collective-permute-done | bytes 860192 | tf_op jit(solution)/shard_map/ppermute | solution.py:505
  731.3 8.7 %collective-permute-done.93 = bf16[560,768]{1,0:T(8,128)(2,1)S(1)} collective-permute-done((bf16[560,768]{1,0:T(8,128)(2,1)S(1)}, bf16[560,768]{1,0:T(8,128)(2,1)S(1)}, u32[]{:S(2)}, u32[]{:S(2)}) %collective-permute-start.93) | collective-permute-done | bytes 860192 | tf_op jit(solution)/shard_map/ppermute | solution.py:505
  (422 shorter events, 403.5 us)
Async XLA Ops:
  7.2 79.4 %all-gather.3.cloned.1.call-start = ((), (), s32[]{:S(2)}) async-start(), calls=%async_computation.2 | async-start | bytes 2359296 | tf_op jit(solution)/shard_map/all_gather | solution.py:724
  33.3 399.9 %reduce-scatter.2.cloned.1.call-start = ((), (), s32[]{:S(2)}) async-start(), calls=%async_computation.1 | async-start | bytes 2359296 | tf_op jit(solution)/shard_map/reduce_scatter | solution.py:824
  33.4 27.9 %collective-permute-start.6 = (bf16[384,1536]{1,0:T(8,128)(2,1)S(1)}, bf16[384,1536]{1,0:T(8,128)(2,1)S(1)}, u32[]{:S(2)}, u32[]{:S(2)}) collective-permute-start(bf16[384,1536]{1,0:T(8,128)(2,1)S(1)} %copy-done.5), channel_id=1, source_target_pairs={{0,2},{1,3},{2,0},{3,1},{4,6},{5,7},{6,4},{7,5},{8,10},{9,11},{10,... | collective-permute-start | bytes 3538952 | tf_op jit(solution)/shard_map/ppermute | solution.py:505
  34.0 27.4 %collective-permute-start.8 = (bf16[384,1536]{1,0:T(8,128)(2,1)S(1)}, bf16[384,1536]{1,0:T(8,128)(2,1)S(1)}, u32[]{:S(2)}, u32[]{:S(2)}) collective-permute-start(bf16[384,1536]{1,0:T(8,128)(2,1)S(1)} %copy-done.5), channel_id=1, source_target_pairs={{0,1},{1,0},{2,3},{3,2},{4,5},{5,4},{6,7},{7,6},{8,9},{9,8},{10,11... | collective-permute-start | bytes 3538952 | tf_op jit(solution)/shard_map/ppermute | solution.py:505
  83.2 27.9 %collective-permute-start.12 = (bf16[384,1536]{1,0:T(8,128)(2,1)S(1)}, bf16[384,1536]{1,0:T(8,128)(2,1)S(1)}, u32[]{:S(2)}, u32[]{:S(2)}) collective-permute-start(bf16[384,1536]{1,0:T(8,128)(2,1)S(1)} %copy-done.4), channel_id=1, source_target_pairs={{0,2},{1,3},{2,0},{3,1},{4,6},{5,7},{6,4},{7,5},{8,10},{9,11},{10,... | collective-permute-start | bytes 3538952 | tf_op jit(solution)/shard_map/ppermute | solution.py:505
  83.7 27.3 %collective-permute-start.13 = (bf16[384,1536]{1,0:T(8,128)(2,1)S(1)}, bf16[384,1536]{1,0:T(8,128)(2,1)S(1)}, u32[]{:S(2)}, u32[]{:S(2)}) collective-permute-start(bf16[384,1536]{1,0:T(8,128)(2,1)S(1)} %copy-done.4), channel_id=1, source_target_pairs={{0,1},{1,0},{2,3},{3,2},{4,5},{5,4},{6,7},{7,6},{8,9},{9,8},{10,11... | collective-permute-start | bytes 3538952 | tf_op jit(solution)/shard_map/ppermute | solution.py:505
  85.1 24.5 %collective-permute-start.14 = (bf16[256,1536]{1,0:T(8,128)(2,1)}, bf16[256,1536]{1,0:T(8,128)(2,1)}, u32[]{:S(2)}, u32[]{:S(2)}) collective-permute-start(bf16[256,1536]{1,0:T(8,128)(2,1)} %collective-permute-done.10.refs_1_.refs_3_), channel_id=1, source_target_pairs={{0,4},{4,0},{8,12},{12,8},{16,20},{20,16},{24,28},{28,24},{1,5},{5... | collective-permute-start | bytes 2359304 | tf_op jit(solution)/shard_map/ppermute | solution.py:505
  207.9 28.7 %collective-permute-start.27 = (bf16[256,384]{1,0:T(8,128)(2,1)}, bf16[256,384]{1,0:T(8,128)(2,1)S(1)}, u32[]{:S(2)}, u32[]{:S(2)}) collective-permute-start(bf16[256,384]{1,0:T(8,128)(2,1)} %get-tuple-element.424), channel_id=1, source_target_pairs={{0,2},{1,3},{2,0},{3,1},{4,6},{5,7},{6,4},{7,5},{8,10},{9,11},{10,... | collective-permute-start | bytes 589832 | tf_op jit(solution)/shard_map/ppermute | solution.py:505
  208.7 27.9 %collective-permute-start.28 = (bf16[256,384]{1,0:T(8,128)(2,1)}, bf16[256,384]{1,0:T(8,128)(2,1)S(1)}, u32[]{:S(2)}, u32[]{:S(2)}) collective-permute-start(bf16[256,384]{1,0:T(8,128)(2,1)} %get-tuple-element.425), channel_id=1, source_target_pairs={{0,1},{1,0},{2,3},{3,2},{4,5},{5,4},{6,7},{7,6},{8,9},{9,8},{10,11... | collective-permute-start | bytes 589832 | tf_op jit(solution)/shard_map/ppermute | solution.py:505
  208.7 27.9 %collective-permute-start.29 = (bf16[256,384]{1,0:T(8,128)(2,1)S(1)}, bf16[256,384]{1,0:T(8,128)(2,1)S(1)}, u32[]{:S(2)}, u32[]{:S(2)}) collective-permute-start(bf16[256,384]{1,0:T(8,128)(2,1)S(1)} %get-tuple-element.426), channel_id=1, source_target_pairs={{0,3},{1,2},{2,1},{3,0},{4,7},{5,6},{6,5},{7,4},{8,11},{9,10},{10,... | collective-permute-start | bytes 589832 | tf_op jit(solution)/shard_map/ppermute | solution.py:505
  210.1 26.5 %collective-permute-start.26 = (bf16[560,768]{1,0:T(8,128)(2,1)}, bf16[560,768]{1,0:T(8,128)(2,1)S(1)}, u32[]{:S(2)}, u32[]{:S(2)}) collective-permute-start(bf16[560,768]{1,0:T(8,128)(2,1)} %get-tuple-element.423), channel_id=1, source_target_pairs={{0,8},{4,12},{24,16},{28,20},{1,9},{5,13},{25,17},{29,21},{2,10},{... | collective-permute-start | bytes 2580488 | tf_op jit(solution)/shard_map/ppermute | solution.py:545
  237.4 24.7 %collective-permute-start.31 = (bf16[512,1536]{1,0:T(8,128)(2,1)}, bf16[512,1536]{1,0:T(8,128)(2,1)}, u32[]{:S(2)}, u32[]{:S(2)}) collective-permute-start(bf16[512,1536]{1,0:T(8,128)(2,1)} %get-tuple-element.439), channel_id=1, source_target_pairs={{0,1},{1,0},{2,3},{3,2},{4,5},{5,4},{6,7},{7,6},{8,9},{9,8},{10,11... | collective-permute-start | bytes 4718600 | tf_op jit(solution)/shard_map/ppermute | solution.py:505
  295.2 29.1 %collective-permute-start.38 = (bf16[560,768]{1,0:T(8,128)(2,1)}, bf16[560,768]{1,0:T(8,128)(2,1)}, u32[]{:S(2)}, u32[]{:S(2)}) collective-permute-start(bf16[560,768]{1,0:T(8,128)(2,1)} %get-tuple-element.465.went.sent), channel_id=1, source_target_pairs={{0,8},{4,12},{24,16},{28,20},{1,9},{5,13},{25,17},{29,21},{2,10},{... | collective-permute-start | bytes 2580488 | tf_op jit(solution)/shard_map/ppermute | solution.py:545
  296.5 27.8 %collective-permute-start.39 = (bf16[560,768]{1,0:T(8,128)(2,1)}, bf16[560,768]{1,0:T(8,128)(2,1)}, u32[]{:S(2)}, u32[]{:S(2)}) collective-permute-start(bf16[560,768]{1,0:T(8,128)(2,1)} %add_convert_fusion.2.summed), channel_id=1, source_target_pairs={{8,16},{12,20},{16,8},{20,12},{9,17},{13,21},{17,9},{21,13},{10,18... | collective-permute-start | bytes 2580488 | tf_op jit(solution)/shard_map/ppermute | solution.py:545
  349.5 41.5 %collective-permute-start.46 = (bf16[512,1536]{1,0:T(8,128)(2,1)}, bf16[512,1536]{1,0:T(8,128)(2,1)}, u32[]{:S(2)}, u32[]{:S(2)}) collective-permute-start(bf16[512,1536]{1,0:T(8,128)(2,1)} %constant_dynamic-update-slice_fusion.2.refs_0_), channel_id=1, source_target_pairs={{0,1},{1,0},{2,3},{3,2},{4,5},{5,4},{6,7},{7,6},{8,9},{9,8},{10,11... | collective-permute-start | bytes 4718600 | tf_op jit(solution)/shard_map/ppermute | solution.py:505
  350.9 36.3 %collective-permute-start.43 = (bf16[560,768]{1,0:T(8,128)(2,1)S(1)}, bf16[560,768]{1,0:T(8,128)(2,1)S(1)}, u32[]{:S(2)}, u32[]{:S(2)}) collective-permute-start(bf16[560,768]{1,0:T(8,128)(2,1)S(1)} %copy-done.36), channel_id=1, source_target_pairs={{0,8},{4,12},{24,16},{28,20},{8,0},{12,4},{16,24},{20,28},{1,9},{5... | collective-permute-start | bytes 2580488 | tf_op jit(solution)/shard_map/ppermute | solution.py:545
  350.9 40.1 %collective-permute-start.44 = (bf16[560,768]{1,0:T(8,128)(2,1)S(1)}, bf16[560,768]{1,0:T(8,128)(2,1)}, u32[]{:S(2)}, u32[]{:S(2)}) collective-permute-start(bf16[560,768]{1,0:T(8,128)(2,1)S(1)} %copy-done.35), channel_id=1, source_target_pairs={{8,16},{12,20},{16,8},{20,12},{9,17},{13,21},{17,9},{21,13},{10,18... | collective-permute-start | bytes 2580488 | tf_op jit(solution)/shard_map/ppermute | solution.py:545
  393.1 29.4 %collective-permute-start.50 = (bf16[512,1536]{1,0:T(8,128)(2,1)}, bf16[512,1536]{1,0:T(8,128)(2,1)}, u32[]{:S(2)}, u32[]{:S(2)}) collective-permute-start(bf16[512,1536]{1,0:T(8,128)(2,1)} %constant_dynamic-update-slice_fusion.4.refs_2_), channel_id=1, source_target_pairs={{0,1},{1,0},{2,3},{3,2},{4,5},{5,4},{6,7},{7,6},{8,9},{9,8},{10,11... | collective-permute-start | bytes 4718600 | tf_op jit(solution)/shard_map/ppermute | solution.py:505
  393.1 26.0 %collective-permute-start.47 = (bf16[560,768]{1,0:T(8,128)(2,1)}, bf16[560,768]{1,0:T(8,128)(2,1)S(1)}, u32[]{:S(2)}, u32[]{:S(2)}) collective-permute-start(bf16[560,768]{1,0:T(8,128)(2,1)} %get-tuple-element.507.sent), channel_id=1, source_target_pairs={{0,8},{4,12},{24,16},{28,20},{8,0},{12,4},{16,24},{20,28},{1,9},{5... | collective-permute-start | bytes 2580488 | tf_op jit(solution)/shard_map/ppermute | solution.py:545
  393.1 26.0 %collective-permute-start.48 = (bf16[560,768]{1,0:T(8,128)(2,1)}, bf16[560,768]{1,0:T(8,128)(2,1)}, u32[]{:S(2)}, u32[]{:S(2)}) collective-permute-start(bf16[560,768]{1,0:T(8,128)(2,1)} %get-tuple-element.508.summed), channel_id=1, source_target_pairs={{8,16},{12,20},{16,8},{20,12},{9,17},{13,21},{17,9},{21,13},{10,18... | collective-permute-start | bytes 2580488 | tf_op jit(solution)/shard_map/ppermute | solution.py:545
  396.5 26.0 %collective-permute-start.49 = (bf16[560,768]{1,0:T(8,128)(2,1)}, bf16[560,768]{1,0:T(8,128)(2,1)}, u32[]{:S(2)}, u32[]{:S(2)}) collective-permute-start(bf16[560,768]{1,0:T(8,128)(2,1)} %get-tuple-element.612.refs_0_), channel_id=1, source_target_pairs={{0,4},{4,0},{8,12},{12,8},{16,20},{20,16},{24,28},{28,24},{1,5},{5... | collective-permute-start | bytes 2580488 | tf_op jit(solution)/shard_map/ppermute | solution.py:505
  422.5 25.7 %collective-permute-start.54 = (bf16[512,1536]{1,0:T(8,128)(2,1)}, bf16[512,1536]{1,0:T(8,128)(2,1)S(1)}, u32[]{:S(2)}, u32[]{:S(2)}) collective-permute-start(bf16[512,1536]{1,0:T(8,128)(2,1)} %get-tuple-element.527), channel_id=1, source_target_pairs={{0,1},{1,0},{2,3},{3,2},{4,5},{5,4},{6,7},{7,6},{8,9},{9,8},{10,11... | collective-permute-start | bytes 4718600 | tf_op jit(solution)/shard_map/ppermute | solution.py:505
  500.9 37.3 %collective-permute-start.70 = (bf16[560,768]{1,0:T(8,128)(2,1)}, bf16[560,768]{1,0:T(8,128)(2,1)S(1)}, u32[]{:S(2)}, u32[]{:S(2)}) collective-permute-start(bf16[560,768]{1,0:T(8,128)(2,1)} %get-tuple-element.585), channel_id=1, source_target_pairs={{0,4},{4,0},{8,12},{12,8},{16,20},{20,16},{24,28},{28,24},{1,5},{5... | collective-permute-start | bytes 2580488 | tf_op jit(solution)/shard_map/ppermute | solution.py:505
  541.9 36.4 %collective-permute-start.74 = (bf16[560,768]{1,0:T(8,128)(2,1)}, bf16[560,768]{1,0:T(8,128)(2,1)}, u32[]{:S(2)}, u32[]{:S(2)}) collective-permute-start(bf16[560,768]{1,0:T(8,128)(2,1)} %fusion.4), channel_id=1, source_target_pairs={{0,4},{4,0},{8,12},{12,8},{16,20},{20,16},{24,28},{28,24},{1,5},{5... | collective-permute-start | bytes 2580488 | tf_op jit(solution)/shard_map/ppermute | solution.py:505
  (142 other events, 1839.6 us)
Sparse Core Ops, SparseCore 0:
  33.4 52.0 all-gather.2
  349.6 83.6 reduce-scatter.1
